TPU v7x, 256 devices: a whole 4x4x8 slice. The times are simulated.
256 devices in a mesh: row: 8 (over x, y_hi), col: 32 (over y_lo, z, core).
Axes of the slice: x: 4, y: 4 (y_hi: 2, y_lo: 2; y = y_hi * 2 + y_lo), z: 8, core: 2. Of those that a mesh axis runs over, the one named last changes fastest.
Arguments:
- embed: float32 [65536, 128], P(('row', 'col')), may hold values from -6 to 6
- cotangent: float32 [65536, 128], P(('col', 'row')), may hold values from -6 to 6
- tile_values: float32 [32, 8, 128, 128, 128], P('col', 'row'), may hold values from 0 to 1
- tile_coords: int32 [2, 32, 8, 128], P(None, 'col', 'row'), may hold values from 0 to 63, as said below
- tile_count: int32 [32, 8], P('col', 'row'), may hold values from 1 to 128, as said below
- row_degree: int32 [65536], P(('col', 'row')), may hold values from 16 to 511
- col_degree: int32 [65536], P(('row', 'col')), may hold values from 16 to 511
Outputs:
- propagated: float32 [65536, 128], P(('col', 'row'))
- embed_grad: float32 [65536, 128], P(('row', 'col'))
Inputs may be any that keep to these rules, and one draw needn't show every extreme that they name: `tile_coords`: within one device block the slots hold distinct tile positions; the first component is below 16 and the second below 64. `tile_count`: some device block has all 128 slots live.
All inputs are finite; a program needn't handle non-finite values.
Results may differ from a plain program's by a relative error of at most 0.0003.
Values sent between devices are 32-bit elements; how exact they have to be, the bound alone decides.
A program may use at most 128 MiB of HBM per device.

v0:
```python
import jax
import jax.numpy as jnp
from jax import lax
from jax.sharding import PartitionSpec as P


def tile_terms(values, rows_at, cols_at, live_mask, panel_tiles, grad_tiles):
    picked = jnp.take(panel_tiles, cols_at, axis=0)
    forward_each = jnp.einsum("tij,tjd->tid", values, picked, precision=lax.Precision.HIGHEST)
    row_hot = (
        (rows_at[None, :] == jnp.arange(grad_tiles.shape[0], dtype=jnp.int32)[:, None])
        & live_mask[None, :]
    ).astype(jnp.float32)
    forward = jnp.einsum("at,tid->aid", row_hot, forward_each, precision=lax.Precision.HIGHEST)
    grad_picked = jnp.take(grad_tiles, rows_at, axis=0)
    backward_each = jnp.einsum("tij,tid->tjd", values, grad_picked, precision=lax.Precision.HIGHEST)
    col_hot = (
        (cols_at[None, :] == jnp.arange(panel_tiles.shape[0], dtype=jnp.int32)[:, None])
        & live_mask[None, :]
    ).astype(jnp.float32)
    backward = jnp.einsum("bt,tjd->bjd", col_hot, backward_each, precision=lax.Precision.HIGHEST)
    return (forward, backward)


def per_device(embed, cotangent, tile_values, tile_coords, tile_count, row_degree, col_degree):
    tile_size = tile_values.shape[-1]
    feature_width = embed.shape[1]
    capacity = tile_values.shape[2]
    values = tile_values[0, 0]
    rows_at = tile_coords[0, 0, 0]
    cols_at = tile_coords[1, 0, 0]
    live_count = tile_count[0, 0]
    scaled = embed * lax.rsqrt(col_degree.astype(jnp.float32))[:, None]
    grad_scaled = cotangent * lax.rsqrt(row_degree.astype(jnp.float32))[:, None]
    embed_panel = lax.all_gather(scaled, "col", axis=0, tiled=True)
    grad_panel = lax.all_gather(grad_scaled, "row", axis=0, tiled=True)
    panel_tiles = embed_panel.reshape(-1, tile_size, feature_width)
    grad_tiles = grad_panel.reshape(-1, tile_size, feature_width)
    live_mask = jnp.arange(capacity, dtype=jnp.int32) < live_count
    forward, backward = tile_terms(values, rows_at, cols_at, live_mask, panel_tiles, grad_tiles)
    summed = lax.psum_scatter(
        forward.reshape(-1, feature_width), "row", scatter_dimension=0, tiled=True
    )
    propagated = summed * lax.rsqrt(row_degree.astype(jnp.float32))[:, None]
    grad_summed = lax.psum_scatter(
        backward.reshape(-1, feature_width), "col", scatter_dimension=0, tiled=True
    )
    embed_grad = grad_summed * lax.rsqrt(col_degree.astype(jnp.float32))[:, None]
    return (propagated, embed_grad)


def solution(mesh):
    return jax.shard_map(
        per_device,
        mesh=mesh,
        in_specs=(
            P(("row", "col"), None),
            P(("col", "row"), None),
            P("col", "row", None, None, None),
            P(None, "col", "row", None),
            P("col", "row"),
            P(("col", "row")),
            P(("row", "col")),
        ),
        out_specs=(P(("col", "row"), None), P(("row", "col"), None)),
        check_vma=False,
    )
```

profile of v0, /device:TPU:1, one launch (start us, length us, event | category | flops | bytes accessed | tf_op | source)
XLA Modules:
  0.0 427.3 jit_solution(3082143181208052741)
XLA Ops:
  7.2 0.0 all-gather.5.cloned.1.call-start
  7.2 0.7 convert_rsqrt_fusion
  7.9 1.7 broadcast_multiply_fusion
  9.6 0.0 all-gather.5.cloned.1.call-update
  9.6 0.0 reduce-scatter.5.cloned.1.call-start
  10.3 0.7 fusion.25
  11.0 0.7 slice_bitcast_fusion
  11.7 0.7 compare_and_fusion
  12.3 53.3 %all-gather.5.cloned.1.call-done = f32[2048,128]{1,0:T(8,128)} async-done(((f32[256,128]{1,0:T(8,128)}), f32[2048,128]{1,0:T(8,128)}) %all-gather.5.cloned.1.call-update) | async-done | bytes 1048592 | tf_op jit(solution)/shard_map/all_gather | solution.py:36
  65.6 5.5 %gather_fusion.1 = f32[128,128,128]{2,1,0:T(8,128)} fusion(f32[16,128,128]{2,1,0:T(8,128)} %bitcast.39, s32[1024]{0:T(1024)S(1)} %pad_clamp_fusion), kind=kCustom, calls=%fused_computation.1 | custom fusion | bytes 16777728 | tf_op jit(solution)/shard_map/jit(_take)/gather | solution.py:15
  71.2 19.5 %fusion.4 = f32[128,128,128]{2,1,0:T(8,128)} fusion(f32[1,1,128,128,128]{4,3,2,1,0:T(8,128)} %param.9, f32[128,128,128]{2,1,0:T(8,128)} %gather_fusion.1, pred[128]{0:T(512)(128)(4,1)S(1)} %get-tuple-element.6), kind=kOutput, calls=%fused_computation.6 | convolution fusion | flops 3223322624 | bytes 25165952 | tf_op jit(solution)/shard_map/tij,tid->tjd/dot_general | solution.py:16
  90.6 9.4 %copy.12 = f32[128,128,128]{1,0,2:T(8,128)} copy(f32[128,128,128]{2,1,0:T(8,128)} %fusion.4) | data formatting | bytes 16777216 | tf_op jit(solution)/shard_map/tij,tid->tjd/dot_general | solution.py:16
  100.0 6.0 %fusion = f32[64,128,128]{2,0,1:T(8,128)S(1)} fusion(f32[128,128,128]{1,0,2:T(8,128)} %copy.12, s32[128]{0:T(128)S(1)} %get-tuple-element.4, pred[128]{0:T(512)(128)(4,1)S(1)} %iota_compare_fusion.2), kind=kOutput, calls=%fused_computation.2 | convolution fusion | flops 1610629120 | bytes 12583552 | tf_op jit(solution)/shard_map/bt,tjd->bjd/dot_general | solution.py:21
  106.0 0.0 copy-start.1
  106.0 0.0 copy-start
  106.0 4.4 %copy.10 = f32[64,128,128]{2,1,0:T(8,128)} copy(f32[64,128,128]{2,0,1:T(8,128)S(1)} %fusion) | data formatting | bytes 8388608 | tf_op jit(solution)/shard_map/bt,tjd->bjd/dot_general | solution.py:21
  110.4 0.0 reduce-scatter.5.cloned.1.call-update
  110.4 0.0 all-gather.3.cloned.1.call-start
  110.5 0.0 copy-done.1
  110.5 120.9 %reduce-scatter.5.cloned.1.call-done = f32[256,128]{1,0:T(8,128)} async-done(((f32[8192,128]{1,0:T(8,128)}), f32[256,128]{1,0:T(8,128)}) %reduce-scatter.5.cloned.1.call-update) | async-done | bytes 131088 | tf_op jit(solution)/shard_map/reduce_scatter | solution.py:45
  231.4 0.0 copy-done
  231.4 1.7 broadcast_multiply_fusion.2
  233.1 0.0 all-gather.3.cloned.1.call-update
  233.1 0.0 reduce-scatter.3.cloned.1.call-start
  233.2 66.8 %all-gather.3.cloned.1.call-done = f32[8192,128]{1,0:T(8,128)} async-done(((f32[256,128]{1,0:T(8,128)}), f32[8192,128]{1,0:T(8,128)}) %all-gather.3.cloned.1.call-update) | async-done | bytes 4194320 | tf_op jit(solution)/shard_map/all_gather | solution.py:35
  300.0 6.5 %gather_fusion = f32[128,128,128]{2,1,0:T(8,128)} fusion(f32[64,128,128]{2,1,0:T(8,128)} %bitcast.40, s32[1024]{0:T(1024)S(1)} %pad_clamp_fusion.1), kind=kCustom, calls=%fused_computation | custom fusion | bytes 16777728 | tf_op jit(solution)/shard_map/jit(_take)/gather | solution.py:8
  306.5 21.2 %fusion.6 = f32[128,128,128]{2,1,0:T(8,128)} fusion(f32[1,1,128,128,128]{4,3,2,1,0:T(8,128)} %param.9, f32[128,128,128]{2,1,0:T(8,128)} %gather_fusion, pred[128]{0:T(512)(128)(4,1)S(1)} %get-tuple-element.7), kind=kOutput, calls=%fused_computation.8 | convolution fusion | flops 3223322624 | bytes 25165952 | tf_op jit(solution)/shard_map/tij,tjd->tid/dot_general | solution.py:9
  327.7 9.4 %copy.11 = f32[128,128,128]{1,0,2:T(8,128)} copy(f32[128,128,128]{2,1,0:T(8,128)} %fusion.6) | data formatting | bytes 16777216 | tf_op jit(solution)/shard_map/tij,tjd->tid/dot_general | solution.py:9
  337.0 5.2 %fusion.2 = f32[16,128,128]{2,0,1:T(8,128)S(1)} fusion(f32[128,128,128]{1,0,2:T(8,128)} %copy.11, s32[128]{0:T(128)S(1)} %get-tuple-element.5, pred[128]{0:T(512)(128)(4,1)S(1)} %iota_compare_fusion.2), kind=kOutput, calls=%fused_computation.4 | convolution fusion | flops 402657280 | bytes 9437824 | tf_op jit(solution)/shard_map/at,tid->aid/dot_general | solution.py:14
  342.2 1.3 copy.9
  343.5 0.0 reduce-scatter.3.cloned.1.call-update
  343.5 75.6 %reduce-scatter.3.cloned.1.call-done = f32[256,128]{1,0:T(8,128)} async-done(((f32[2048,128]{1,0:T(8,128)}), f32[256,128]{1,0:T(8,128)}) %reduce-scatter.3.cloned.1.call-update) | async-done | bytes 131088 | tf_op jit(solution)/shard_map/reduce_scatter | solution.py:41
  419.1 1.7 broadcast_multiply_fusion.1
  (4 shorter events, 0.0 us)
Async XLA Ops:
  7.2 58.5 %all-gather.5.cloned.1.call-start = ((), (), s32[]{:S(2)}) async-start(), calls=%async_computation.4 | async-start | bytes 1179648 | tf_op jit(solution)/shard_map/all_gather | solution.py:36
  9.6 221.8 %reduce-scatter.5.cloned.1.call-start = ((), (), s32[]{:S(2)}) async-start(), calls=%async_computation.5 | async-start | bytes 4325376 | tf_op jit(solution)/shard_map/reduce_scatter | solution.py:45
  106.0 4.5 %copy-start.1 = (s32[256]{0:T(256)S(1)}, s32[256]{0:T(256)}, u32[]{:S(2)}) copy-start(s32[256]{0:T(256)} %param.13) | copy-start | bytes 3076
  106.0 125.4 %copy-start = (f32[256,128]{1,0:T(8,128)S(1)}, f32[256,128]{1,0:T(8,128)}, u32[]{:S(2)}) copy-start(f32[256,128]{1,0:T(8,128)} %param.7) | copy-start | bytes 393220
  110.4 189.5 %all-gather.3.cloned.1.call-start = ((), (), s32[]{:S(2)}) async-start(), calls=%async_computation.2 | async-start | bytes 4325376 | tf_op jit(solution)/shard_map/all_gather | solution.py:35
  233.1 186.0 %reduce-scatter.3.cloned.1.call-start = ((), (), s32[]{:S(2)}) async-start(), calls=%async_computation.3 | async-start | bytes 1179648 | tf_op jit(solution)/shard_map/reduce_scatter | solution.py:41
Sparse Core Ops, SparseCore 0:
  11.2 54.4 all-gather.4
  110.6 120.7 reduce-scatter.4
  233.8 66.1 all-gather.2
  343.6 75.4 reduce-scatter.2
where the time goes:
time: 429 us; the launch traced here: 427 us
  waiting for transfers between devices  317 us (74%)
  matrix products  51.9 us (12%)
  local copies, waits for them, and re-layouts  37.1 us (9%)
  between operations  14.5 us (3%)
  other arithmetic  7.09 us (2%)
    reduce_scatter x1, waiting for transfers between devices, per_device(): lax.psum_scatter(backward.reshape(-1, feature_width), 'col', scatter_dime...  121 us
    reduce_scatter x1, waiting for transfers between devices, per_device(): lax.psum_scatter(forward.reshape(-1, feature_width), 'row', scatter_dimen...  75.6 us
    all_gather x1, waiting for transfers between devices, per_device(): embed_panel = lax.all_gather(scaled, 'col', axis=0, tiled=True)  66.8 us
    all_gather x1, waiting for transfers between devices, per_device(): grad_panel = lax.all_gather(grad_scaled, 'row', axis=0, tiled=True)  53.3 us
    dot_general x1, matrix products, tile_terms(): jnp.einsum('tij,tjd->tid', values, picked, precision=lax.Precision.HIGHEST)  21.2 us
    dot_general x1, matrix products, tile_terms(): jnp.einsum('tij,tid->tjd', values, grad_picked, precision=lax.Precision.H...  19.5 us
    dot_general x1, local copies, waits for them, and re-layouts, tile_terms(): jnp.einsum('tij,tid->tjd', values, grad_picked, precision=lax.Precision.H...  9.36 us
    dot_general x1, local copies, waits for them, and re-layouts, tile_terms(): jnp.einsum('tij,tjd->tid', values, picked, precision=lax.Precision.HIGHEST)  9.36 us
  transfers between devices with their start and end apart: 4, of which 4 were waited for; matrix products, arithmetic and copies ran while one was open for 0% of the time, Pallas kernels for 0%

commit v1 on v0

v1 whole, which is shorter than its diff:
```python
import jax
import jax.numpy as jnp
from jax import lax
from jax.experimental import pallas as pl
from jax.experimental.pallas import tpu as pltpu
from jax.sharding import PartitionSpec as P

MESH = pl.DeviceIdType.MESH
F32 = jnp.float32
BF16 = jnp.bfloat16
T = 128
SLOTS = 128
NX, NZ = 4, 8
N_COPIES = 156


class Comm:
    def __init__(self, send_sems, recv_sems):
        self.send_sems, self.recv_sems, self.n, self.all = send_sems, recv_sems, 0, []

    def send(self, src, dst, dev, land=None):
        copy = pltpu.make_async_remote_copy(
            src_ref=src,
            dst_ref=dst,
            send_sem=self.send_sems.at[self.n],
            recv_sem=self.recv_sems.at[self.n],
            device_id=dev,
            device_id_type=MESH,
        )
        copy.start()
        back = pltpu.make_async_remote_copy(
            src_ref=src,
            dst_ref=dst if land is None else land,
            send_sem=self.send_sems.at[self.n],
            recv_sem=self.recv_sems.at[self.n],
            device_id=dev,
            device_id_type=MESH,
        )
        self.n += 1
        self.all.append(copy)
        return back.wait_recv

    def drain(self):
        for copy in self.all:
            copy.wait_send()


def split(value):
    high = value.astype(BF16)
    return high, (value - high.astype(F32)).astype(BF16)


def kernel(
    idx, embed, cot, rdeg, cdeg, values,
    prop_out, grad_out,
    panel, pairs, vraw, vpair, fwd_each, bwd_each, part, from_core, ring, from_y,
    gpanel, gpair, fpart, xring, relay, frelay, from_yh,
    send_sems, recv_sems, load_sems,
):
    row, col = lax.axis_index("row"), lax.axis_index("col")
    x, yh = lax.div(row, 2), lax.rem(row, 2)
    core, chip = lax.rem(col, 2), lax.div(col, 2)
    yl, z = lax.div(chip, NZ), lax.rem(chip, NZ)
    turn = 1 - 2 * core

    def zat(d):
        return lax.rem(z + turn * d + NZ, NZ)

    def xat(d):
        return lax.rem(x + turn * d + NX, NX)

    def colof(y, zz, c):
        return (y * NZ + zz) * 2 + c

    def ctile(other, d, h, c=None, sign=1):
        y = 1 - yl if other else yl
        return colof(y, zat(sign * d), core if c is None else c) * 2 + h

    def rtile(other, d, h):
        return (xat(d) * 2 + (1 - yh if other else yh)) * 2 + h

    partner = (row, col + turn)
    za = (row, colof(yl, zat(1), core))
    zb = (row, colof(yl, zat(-1), core))
    ypair = (row, colof(1 - yl, z, core))
    cross = (x * 2 + 1 - yh, colof(1 - yl, z, core))
    xa = (xat(1) * 2 + yh, col)
    xb = (xat(-1) * 2 + yh, col)
    first_pair = 1 - core
    hop1 = (x * 2 + (yh * first_pair + (1 - yh) * core), colof(1 - yl, z, core))
    hop2 = (x * 2 + (yh * core + (1 - yh) * first_pair), colof(1 - yl, z, core))
    relay_yh = yh * first_pair + (1 - yh) * core

    loads = []
    group = SLOTS // 8
    for g in range(8):
        piece = pl.ds(g * group, group)
        load = pltpu.make_async_copy(values.at[piece], vraw.at[piece], load_sems.at[g])
        load.start()
        loads.append(load)

    for h in range(2):
        half = pl.ds(h * T, T)
        rs = lax.rsqrt(rdeg[pl.ds(h, 1), :].astype(F32))
        cs = lax.rsqrt(cdeg[pl.ds(h, 1), :].astype(F32))
        gpanel[rtile(0, 0, h)] = cot[half, :].T * rs
        panel[ctile(0, 0, h)] = (embed[half, :].T * cs).T
    fwd_each[SLOTS] = jnp.zeros((T, T), F32)
    bwd_each[SLOTS] = jnp.zeros((T, T), F32)

    barrier = pltpu.get_barrier_semaphore()
    for dev in (partner, za, zb, ypair, cross, xa, xb):
        pl.semaphore_signal(barrier, inc=1, device_id=dev, device_id_type=MESH)
    pl.semaphore_wait(barrier, 7)

    comm = Comm(send_sems, recv_sems)

    def share(ref, tile, dev, land):
        return comm.send(ref.at[tile], ref.at[tile], dev, ref.at[land])

    to_core = []

    def col_core(tile, land):
        to_core.append(share(panel, tile, partner, land))

    def key_land(other, d, h):
        return ctile(other, d, h, 1 - core, -1)

    relayed = [
        comm.send(gpanel.at[rtile(0, 0, h)], relay.at[h], hop1) for h in range(2)
    ]
    xa1, xb1 = {}, {}
    for h in range(2):
        xa1[0, h] = share(gpanel, rtile(0, 0, h), xa, rtile(0, -1, h))
        xb1[0, h] = share(gpanel, rtile(0, 0, h), xb, rtile(0, 1, h))
    y_first = share(panel, ctile(0, 0, 0), ypair, ctile(1, 0, 0))
    za_got, zb_got, y_got = {}, {}, {}

    def z_send(p, k):
        other, h = ((0, 0), (0, 1), (1, 0))[p]
        if k < 4:
            za_got[k + 1, p] = share(panel, ctile(other, -k, h), za, ctile(other, -k - 1, h))
        if k < 3:
            zb_got[k + 1, p] = share(panel, ctile(other, k, h), zb, ctile(other, k + 1, h))

    z_send(0, 0)
    z_send(1, 0)
    y_got[0] = share(panel, ctile(0, 0, 1), ypair, ctile(1, 0, 1))
    for h in range(2):
        col_core(ctile(0, 0, h), key_land(0, 0, h))

    def ev_relay():
        for h in range(2):
            relayed[h]()
        for h in range(2):
            tile = (x * 2 + relay_yh) * 2 + h
            relayed[h] = comm.send(
                relay.at[h], gpanel.at[tile], hop2, gpanel.at[rtile(1, 0, h)]
            )

    def ev_y_first():
        y_first()
        z_send(2, 0)
        col_core(ctile(1, 0, 0), key_land(1, 0, 0))

    def ev_z(k, p):
        def run():
            other, h = ((0, 0), (0, 1), (1, 0))[p]
            za_got[k, p]()
            if k < 4:
                zb_got[k, p]()
            if k < 4:
                z_send(p, k)
            signs = (-1, 1) if k < 4 else (-1,)
            for s in signs:
                tile = ctile(other, s * k, h)
                if p == 1:
                    y_got[s * k] = share(panel, tile, ypair, ctile(1, s * k, 1))
                col_core(tile, key_land(other, s * k, h))

        return run

    def ev_y(d):
        def run():
            y_got[d]()
            col_core(ctile(1, d, 1), key_land(1, d, 1))

        return run

    def ev_x_other():
        for h in range(2):
            relayed[h]()
            xa1[1, h] = share(gpanel, rtile(1, 0, h), xa, rtile(1, -1, h))
            xb1[1, h] = share(gpanel, rtile(1, 0, h), xb, rtile(1, 1, h))

    xa2 = {}

    def ev_x(other):
        def run():
            for h in range(2):
                xa1[other, h]()
                xa2[other, h] = share(gpanel, rtile(other, -1, h), xa, rtile(other, -2, h))
                xb1[other, h]()

        return run

    def ev_x_end():
        for key in ((0, 0), (0, 1), (1, 0), (1, 1)):
            xa2[key]()

    def ev_core_end():
        for wait in to_core:
            wait()

    def do_split(g):
        def run():
            loads[g].wait()

            def body(i, carry):
                for u in range(2):
                    t = g * group + i * 2 + u
                    high, low = split(vraw[t])
                    vpair[t, pl.ds(0, T), :] = high
                    vpair[t, pl.ds(T, T), :] = low
                return carry

            lax.fori_loop(0, group // 2, body, 0)

        return run

    def do_gsplit():
        def body(r, carry):
            high, low = split(gpanel[r])
            gpair[r, pl.ds(0, T), :] = high
            gpair[r, pl.ds(T, T), :] = low
            return carry

        lax.fori_loop(0, 4 * NX, body, 0)

    def do_bwd(g):
        def run():
            def body(i, carry):
                for u in range(4):
                    t = g * group + i * 4 + u
                    g2 = gpair[idx[0, t]]
                    out = jnp.dot(
                        jnp.concatenate([g2, g2], axis=1), vpair[t], preferred_element_type=F32
                    )
                    bwd_each[t] = out[:T] + out[T:] + bwd_each[idx[3, t]]
                return carry

            lax.fori_loop(0, group // 4, body, 0)

        return run

    def do_ssplit():
        def body(c, carry):
            high, low = split(panel[c])
            pairs[c, :, pl.ds(0, T)] = high
            pairs[c, :, pl.ds(T, T)] = low
            return carry

        lax.fori_loop(0, 8 * NZ, body, 0)

    def do_fwd(g):
        def run():
            def body(i, carry):
                for u in range(4):
                    t = g * group + i * 4 + u
                    s2 = pairs[idx[1, t]]
                    v2 = jnp.concatenate([vpair[t, pl.ds(0, T), :], vpair[t, pl.ds(T, T), :]], axis=1)
                    out = jnp.dot(
                        v2, jnp.concatenate([s2, s2], axis=0), preferred_element_type=F32
                    )
                    fwd_each[t] = out[:, :T] + out[:, T:] + fwd_each[idx[2, t]]
                return carry

            lax.fori_loop(0, group // 4, body, 0)

        return run

    plan = [
        ev_y_first, do_split(0),
        ev_relay, do_split(1),
        ev_z(1, 0), do_split(2), ev_z(1, 1), do_split(3),
        ev_x(0), do_split(4), ev_x_other, do_split(5), ev_z(1, 2), ev_y(0), do_split(6),
        ev_z(2, 0), do_split(7), ev_z(2, 1), ev_y(-1), ev_y(1),
        ev_x(1), ev_z(2, 2), ev_x_end, do_gsplit,
        do_bwd(0), ev_z(3, 0), do_bwd(1), ev_z(3, 1), do_bwd(2), ev_y(-2), ev_y(2),
        do_bwd(3), ev_z(3, 2), do_bwd(4), ev_z(4, 0), do_bwd(5), ev_z(4, 1), ev_y(-3), ev_y(3),
        do_bwd(6), ev_z(4, 2), ev_y(-4), do_bwd(7),
    ]
    for step in plan:
        step()

    def pick(tile, each, last):
        part[tile] = each[last]

    order = (-4, 4)
    need = [(other, d, h) for d in (4, 3, -3, 2, -2, 1, -1, 0) for other, h in ((0, 0), (1, 0), (1, 1), (0, 1))]
    core_got = {}
    for n, (other, d, h) in enumerate(need):
        tile = ctile(other, d, h, 1 - core, -1)
        part[tile] = bwd_each[idx[5, tile]]
        core_got[other, d, h] = comm.send(part.at[tile], from_core.at[n], partner)
    where = {key: n for n, key in enumerate(need)}
    own_y, a_got, b_got = {}, {}, {}

    def ring_send(p, d, sign, slot, got):
        other, h = ((0, 0), (1, 0), (0, 1))[p]
        got[p, slot] = comm.send(
            part.at[ctile(other, d, h)], ring.at[slot * 3 + p], za if sign > 0 else zb
        )

    def merge(other, d, h):
        tile = ctile(other, d, h)
        core_got[other, d, h]()
        part[tile] = bwd_each[idx[5, tile]] + from_core[where[other, d, h]]

    def ev_merge(d):
        def run():
            for other, h in ((0, 0), (1, 0), (1, 1), (0, 1)):
                merge(other, d, h)
                if (other, h) == (1, 1):
                    own_y[d] = comm.send(part.at[ctile(1, d, 1)], from_y.at[d % NZ], ypair)
                if d == 4 and h == 0:
                    ring_send(other, 4, 1, 3, a_got)
                if d == -3 and h == 0:
                    ring_send(other, -3, -1, 6, b_got)

        return run

    def ev_merge_y(d):
        def run():
            own_y[d]()
            part[ctile(0, d, 1)] += from_y[d % NZ]
            if d == 4:
                ring_send(2, 4, 1, 3, a_got)
            if d == -3:
                ring_send(2, -3, -1, 6, b_got)

        return run

    def ev_a(p, left):
        def run():
            other, h = ((0, 0), (1, 0), (0, 1))[p]
            a_got[p, left]()
            part[ctile(other, left, h)] += ring[left * 3 + p]
            if left:
                ring_send(p, left, 1, left - 1, a_got)

        return run

    def ev_b(p, left):
        def run():
            other, h = ((0, 0), (1, 0), (0, 1))[p]
            b_got[p, 4 + left]()
            part[ctile(other, -left, h)] += ring[(4 + left) * 3 + p]
            if left:
                ring_send(p, -left, -1, 4 + left - 1, b_got)

        return run

    def ev_grad_y():
        own_y["end"] = comm.send(part.at[ctile(1, 0, 0)], from_y.at[NZ], ypair)

    def ev_grad_end():
        own_y["end"]()
        for h in range(2):
            total = part[ctile(0, 0, h)]
            if h == 0:
                total = total + from_y[NZ]
            cs = lax.rsqrt(cdeg[pl.ds(h, 1), :].astype(F32))
            grad_out[pl.ds(h * T, T), :] = (total * cs).T

    fa, fb = {}, {}

    def ev_f_start():
        for r in range(4 * NX):
            fpart[r] = fwd_each[idx[4, r]]
        for other in (1, 0):
            for h in range(2):
                fa[other, h] = comm.send(fpart.at[rtile(other, 2, h)], xring.at[other * 2 + h], xa)
                fb[other, h] = comm.send(fpart.at[rtile(other, -1, h)], xring.at[4 + other * 2 + h], xb)

    def ev_f_mid(other):
        def run():
            for h in range(2):
                fa[other, h]()
                fpart[rtile(other, 1, h)] += xring[other * 2 + h]
                fa[other, h] = comm.send(
                    fpart.at[rtile(other, 1, h)], xring.at[8 + other * 2 + h], xa
                )

        return run

    def ev_f_last(other):
        def run():
            for h in range(2):
                fa[other, h]()
                fb[other, h]()
                fpart[rtile(other, 0, h)] += xring[4 + other * 2 + h] + xring[8 + other * 2 + h]
                if other:
                    relayed[h] = comm.send(fpart.at[rtile(1, 0, h)], frelay.at[h], hop1)

        return run

    def ev_f_relay():
        for h in range(2):
            relayed[h]()
            relayed[h] = comm.send(frelay.at[h], from_yh.at[h], hop2)

    def ev_f_end():
        for h in range(2):
            relayed[h]()
            rs = lax.rsqrt(rdeg[pl.ds(h, 1), :].astype(F32))
            total = fpart[rtile(0, 0, h)] + from_yh[h]
            prop_out[pl.ds(h * T, T), :] = (total.T * rs).T

    plan = [
        ev_merge(4), ev_merge(3), ev_merge(-3), ev_merge_y(4), ev_merge_y(3), ev_merge_y(-3),
        ev_merge(2), ev_merge(-2), ev_merge_y(2), ev_merge_y(-2),
        ev_core_end, do_ssplit,
        ev_a(0, 3), ev_b(0, 2), ev_a(1, 3), ev_b(1, 2),
        ev_merge(1), ev_merge(-1), ev_merge_y(1), ev_merge_y(-1), ev_merge(0), ev_merge_y(0),
        do_fwd(0), ev_a(2, 3), ev_b(2, 2),
        do_fwd(1), ev_a(0, 2), ev_b(0, 1), do_fwd(2), ev_a(1, 2), ev_b(1, 1),
        do_fwd(3), ev_a(2, 2), ev_b(2, 1), do_fwd(4), do_fwd(5), ev_a(0, 1), ev_b(0, 0),
        do_fwd(6), ev_a(1, 1), ev_b(1, 0), do_fwd(7), ev_f_start,
        ev_a(2, 1), ev_b(2, 0), ev_f_mid(1), ev_f_mid(0), ev_a(1, 0), ev_grad_y, ev_a(0, 0),
        ev_f_last(1), ev_a(2, 0), ev_f_relay, ev_f_last(0), ev_grad_end, ev_f_end,
    ]
    for step in plan:
        step()
    comm.drain()


def tables(coords, count):
    rows, cols = coords[0, 0, 0], coords[1, 0, 0]
    slot = jnp.arange(SLOTS, dtype=jnp.int32)
    live = slot < count[0, 0]

    def latest(asked, below, keys):
        hit = (asked[:, None] == keys[None, :]) & live[None, :] & (slot[None, :] < below[:, None])
        best = jnp.max(jnp.where(hit, slot[None, :], -1), axis=1)
        return jnp.where(best < 0, SLOTS, best)

    full = jnp.full((SLOTS,), SLOTS, jnp.int32)
    return jnp.stack([
        rows, cols,
        latest(rows, slot, rows), latest(cols, slot, cols),
        latest(slot, full, rows), latest(slot, full, cols),
    ])


def per_device(embed, cotangent, tile_values, tile_coords, tile_count, row_degree, col_degree):
    vmem = pl.BlockSpec(memory_space=pltpu.VMEM)
    tile = lambda n, dtype=F32, a=T, b=T: pltpu.VMEM((n, a, b), dtype)
    return pl.pallas_call(
        kernel,
        out_shape=(jax.ShapeDtypeStruct((2 * T, T), F32), jax.ShapeDtypeStruct((2 * T, T), F32)),
        in_specs=[pl.BlockSpec(memory_space=pltpu.SMEM), vmem, vmem, vmem, vmem, pl.BlockSpec(memory_space=pl.ANY)],
        out_specs=(vmem, vmem),
        scratch_shapes=[
            tile(64), tile(64, BF16, T, 2 * T), tile(SLOTS), tile(SLOTS, BF16, 2 * T, T),
            tile(SLOTS + 1), tile(SLOTS + 1), tile(64), tile(32), tile(21), tile(9),
            tile(16), tile(16, BF16, 2 * T, T), tile(16), tile(12), tile(2), tile(2), tile(2),
            pltpu.SemaphoreType.DMA((N_COPIES,)),
            pltpu.SemaphoreType.DMA((N_COPIES,)),
            pltpu.SemaphoreType.DMA((8,)),
        ],
        compiler_params=pltpu.CompilerParams(
            collective_id=0, has_side_effects=True, vmem_limit_bytes=62 * 1024 * 1024
        ),
    )(
        tables(tile_coords, tile_count), embed, cotangent,
        row_degree.reshape(2, T), col_degree.reshape(2, T), tile_values[0, 0],
    )


def solution(mesh):
    return jax.shard_map(
        per_device,
        mesh=mesh,
        in_specs=(
            P(("row", "col"), None),
            P(("col", "row"), None),
            P("col", "row", None, None, None),
            P(None, "col", "row", None),
            P("col", "row"),
            P(("col", "row")),
            P(("row", "col")),
        ),
        out_specs=(P(("col", "row"), None), P(("row", "col"), None)),
        check_vma=False,
    )
```

time: 429 us -> 92.6 us (0.22)
  the two profiles are of different devices: /device:TPU:1 before, /device:TPU:4 now
where the time goes in v1:
time: 92.6 us; the launch traced here: 92.4 us
  Pallas kernels  86.5 us (93%)
  local copies, waits for them, and re-layouts  4.42 us (5%)
  between operations  1.32 us (1%)
    pallas_call x1, Pallas kernels, per_device(): pl.pallas_call(kernel, out_shape=(jax.ShapeDtypeStruct((2 * T, T), F32),...  86.5 us
    unnamed x2, local copies, waits for them, and re-layouts  3.14 us

profile of v1, /device:TPU:4, one launch (start us, length us, event | category | flops | bytes accessed | tf_op | source)
XLA Modules:
  0.0 92.4 jit_solution(17216110255287978033)
XLA Ops:
  1.3 0.7 slice_bitcast_fusion.2
  2.0 0.2 select_reduce_fusion
  2.2 0.6 stack.2.idx
  2.8 86.5 %shard_map.86 = (f32[256,128]{1,0:T(8,128)}, f32[256,128]{1,0:T(8,128)}) custom-call(s32[6,128]{1,0:T(8,128)} %stack.2.idx, f32[256,128]{1,0:T(8,128)} %embed.1, f32[256,128]{1,0:T(8,128)} %cot.1, s32[2,128]{1,0:T(2,128)} %bitcast.22, s32[2,128]{1,0:T(2,128)} %bitcast.23, f32[128,128,128]{2,1,0:T(8,128)} %bitcast.21), custom_call_target="tpu_custom_call" | custom-call | tf_op jit(solution)/shard_map/pallas_call | solution.py:459
  89.3 1.6 %copy.12 = f32[256,128]{1,0:T(8,128)} copy(f32[256,128]{1,0:T(8,128)} %get-tuple-element.16) | data formatting | bytes 262144
  90.9 1.6 %copy.13 = f32[256,128]{1,0:T(8,128)} copy(f32[256,128]{1,0:T(8,128)} %get-tuple-element.17) | data formatting | bytes 262144
  (4 shorter events, 0.0 us)

commit v2 on v1

v2 whole, which is shorter than its diff:
```python
import jax
import jax.numpy as jnp
from jax import lax
from jax.experimental import pallas as pl
from jax.experimental.pallas import tpu as pltpu
from jax.sharding import PartitionSpec as P

MESH = pl.DeviceIdType.MESH
F32 = jnp.float32
BF16 = jnp.bfloat16
T = 128
SLOTS = 128
NX, NZ = 4, 8
UNROLL = 16
VMEM_LIMIT = 58 * 1024 * 1024
N_RECV = 83
N_AG = N_RS = 76


class Comm:
    def __init__(self, send_sem, recv_sems):
        self.send_sem, self.recv_sems, self.n, self.tiles = send_sem, recv_sems, 0, [0, 0]
        self.phase = 0

    def slot(self):
        self.n += 1
        return self.n - 1

    def copy(self, src, dst, dev, slot):
        return pltpu.make_async_remote_copy(
            src_ref=src,
            dst_ref=dst,
            send_sem=self.send_sem.at[self.phase],
            recv_sem=self.recv_sems.at[slot],
            device_id=dev,
            device_id_type=MESH,
        )

    def send(self, src, dst, dev, land=None, slot=None, n=1):
        slot = self.slot() if slot is None else slot
        self.copy(src, dst, dev, slot).start()
        self.tiles[self.phase] += n
        return lambda: self.copy(src, dst if land is None else land, dev, slot).wait_recv()


def split(value):
    high = value.astype(BF16)
    return high, (value - high.astype(F32)).astype(BF16)


def kernel(
    embed_hbm, cot_hbm, rdeg_hbm, cdeg_hbm, coords_hbm, count_hbm, values,
    out,
    embed, cot, rdeg, cdeg, coords, count, table, idx,
    panel, pairs, vraw, vpair, fwd_each, bwd_each, part, from_core, ring, from_y,
    gpanel, gpair, fpart, xring, from_yh,
    send_sem, recv_sems, load_sems,
):
    row, col = lax.axis_index("row"), lax.axis_index("col")
    x, yh = lax.div(row, 2), lax.rem(row, 2)
    core, chip = lax.rem(col, 2), lax.div(col, 2)
    yl, z = lax.div(chip, NZ), lax.rem(chip, NZ)
    turn = 1 - 2 * core

    def zat(d):
        return lax.rem(z + turn * d + NZ, NZ)

    def xat(d):
        return lax.rem(x + turn * d + NX, NX)

    def colof(y, zz, c):
        return (y * NZ + zz) * 2 + c

    def ctile(other, d, h, c=None, sign=1):
        y = 1 - yl if other else yl
        return colof(y, zat(sign * d), core if c is None else c) * 2 + h

    def rtile(other, d, h):
        return (xat(d) * 2 + (1 - yh if other else yh)) * 2 + h

    partner = (row, col + turn)
    za = (row, colof(yl, zat(1), core))
    zb = (row, colof(yl, zat(-1), core))
    ypair = (row, colof(1 - yl, z, core))
    ypeer = (x * 2 + 1 - yh, col)
    xa = (xat(1) * 2 + yh, col)
    xb = (xat(-1) * 2 + yh, col)

    barrier = pltpu.get_barrier_semaphore()
    for dev in (za, zb, xa, xb, ypair, ypeer, partner):
        pl.semaphore_signal(barrier, inc=1, device_id=dev, device_id_type=MESH)

    inputs = []
    for n, (src, dst) in enumerate((
        (cot_hbm, cot), (rdeg_hbm, rdeg), (embed_hbm, embed), (cdeg_hbm, cdeg), (coords_hbm, coords), (count_hbm, count)
    )):
        load = pltpu.make_async_copy(src, dst, load_sems.at[n])
        load.start()
        inputs.append(load)
    loads = []
    group = SLOTS // 8
    for g in range(4):
        piece = pl.ds(g * 2 * group, 2 * group)
        load = pltpu.make_async_copy(values.at[piece], vraw.at[piece], load_sems.at[6 + g])
        load.start()
        loads.append(load)
    for load in inputs:
        load.wait()

    for h in range(2):
        half = pl.ds(h * T, T)
        rs = lax.rsqrt(rdeg[pl.ds(h, 1), :].astype(F32))
        cs = lax.rsqrt(cdeg[pl.ds(h, 1), :].astype(F32))
        gpanel[rtile(0, 0, h)] = cot[half, :].T * rs
        panel[ctile(0, 0, h)] = (embed[half, :].T * cs).T
    pl.semaphore_wait(barrier, 7)

    comm = Comm(send_sem, recv_sems)

    def share(ref, tile, dev, land, n=1, slot=None):
        if n > 1:
            return comm.send(ref.at[pl.ds(tile, n)], ref.at[pl.ds(tile, n)], dev, ref.at[pl.ds(land, n)], slot, n)
        return comm.send(ref.at[tile], ref.at[tile], dev, ref.at[land], slot)

    core_slot = comm.slot()

    def col_core(tile):
        comm.send(panel.at[tile], panel.at[tile], partner, slot=core_slot)

    got_yh = share(gpanel, rtile(0, 0, 0), ypeer, rtile(1, 0, 0), 2)
    xa1, xb1, xa2 = {}, {}, {}
    xa1[0] = share(gpanel, rtile(0, 0, 0), xa, rtile(0, -1, 0), 2)
    xb1[0] = share(gpanel, rtile(0, 0, 0), xb, rtile(0, 1, 0), 2)
    za_got, zb_got, y_got = {}, {}, {}
    PIECES = ((0, 0), (0, 1), (1, 0))

    def z_send(p, k):
        other, h = PIECES[p]
        if k < 4:
            za_got[k + 1, p] = share(panel, ctile(other, -k, h), za, ctile(other, -k - 1, h))
        if k < 3:
            zb_got[k + 1, p] = share(panel, ctile(other, k, h), zb, ctile(other, k + 1, h))

    z_send(0, 0)
    y_first = share(panel, ctile(0, 0, 0), ypair, ctile(1, 0, 0))
    z_send(1, 0)
    y_got[0] = share(panel, ctile(0, 0, 1), ypair, ctile(1, 0, 1))
    for h in range(2):
        col_core(ctile(0, 0, h))

    sub = lax.broadcasted_iota(jnp.int32, (T, T), 0)
    lane = lax.broadcasted_iota(jnp.int32, (T, T), 1)
    live = sub < count[0, 0]

    def latest(hit):
        best = jnp.max(jnp.where(hit & live, sub, -1), axis=0, keepdims=True)
        return jnp.where(best < 0, SLOTS, best)

    for n in range(2):
        key = jnp.broadcast_to(coords[pl.ds(n, 1), :], (T, T))
        down = key.T
        table[pl.ds(n, 1), :] = coords[pl.ds(n, 1), :]
        table[pl.ds(2 + n, 1), :] = latest((down == key) & (sub < lane))
        table[pl.ds(4 + n, 1), :] = latest(down == lane)
    to_smem = pltpu.make_async_copy(table, idx, load_sems.at[10])
    to_smem.start()
    fwd_each[SLOTS] = jnp.zeros((T, T), F32)
    bwd_each[SLOTS] = jnp.zeros((T, T), F32)

    def ev_row_y():
        got_yh()
        xa1[1] = share(gpanel, rtile(1, 0, 0), xa, rtile(1, -1, 0), 2)
        xb1[1] = share(gpanel, rtile(1, 0, 0), xb, rtile(1, 1, 0), 2)

    def ev_x(other):
        def run():
            xa1[other]()
            xa2[other] = share(gpanel, rtile(other, -1, 0), xa, rtile(other, -2, 0), 2)
            xb1[other]()

        return run

    def ev_x_end():
        xa2[0]()
        xa2[1]()

    def ev_y_first():
        y_first()
        z_send(2, 0)
        col_core(ctile(1, 0, 0))

    def ev_z(k, p):
        def run():
            other, h = PIECES[p]
            za_got[k, p]()
            if k < 4:
                zb_got[k, p]()
                z_send(p, k)
            for s in (-1, 1) if k < 4 else (-1,):
                tile = ctile(other, s * k, h)
                if p == 1:
                    y_got[s * k] = share(panel, tile, ypair, ctile(1, s * k, 1))
                col_core(tile)

        return run

    def ev_y(d):
        def run():
            y_got[d]()
            col_core(ctile(1, d, 1))

        return run

    def ev_core_end():
        comm.copy(panel.at[pl.ds(0, 32)], panel.at[pl.ds(0, 32)], partner, core_slot).wait_recv()

    def do_split(g):
        def run():
            if g % 2 == 0:
                loads[g // 2].wait()

            def body(i, carry):
                for u in range(2):
                    t = g * group + i * 2 + u
                    high, low = split(vraw[t])
                    vpair[t, pl.ds(0, T), :] = high
                    vpair[t, pl.ds(T, T), :] = low
                return carry

            lax.fori_loop(0, group // 2, body, 0)

        return run

    def do_gsplit():
        to_smem.wait()

        def body(r, carry):
            high, low = split(gpanel[r])
            gpair[r, pl.ds(0, T), :] = high
            gpair[r, pl.ds(T, T), :] = low
            return carry

        lax.fori_loop(0, 4 * NX, body, 0)

    def do_bwd(g):
        def run():
            def body(i, carry):
                for u in range(UNROLL):
                    t = g * group + i * UNROLL + u
                    g2 = gpair[idx[0, t]]
                    res = jnp.dot(
                        jnp.concatenate([g2, g2], axis=1), vpair[t], preferred_element_type=F32
                    )
                    bwd_each[t] = res[:T] + res[T:] + bwd_each[idx[3, t]]
                return carry

            lax.fori_loop(0, group // UNROLL, body, 0)

        return run

    def do_ssplit():
        def body(c, carry):
            for u in range(2):
                high, low = split(panel[c * 2 + u])
                pairs[c * 2 + u, :, pl.ds(0, T)] = high
                pairs[c * 2 + u, :, pl.ds(T, T)] = low
            return carry

        lax.fori_loop(0, 4 * NZ, body, 0)

    def do_fwd(g):
        def run():
            def body(i, carry):
                for u in range(UNROLL):
                    t = g * group + i * UNROLL + u
                    s2 = pairs[idx[1, t]]
                    v2 = jnp.concatenate([vpair[t, pl.ds(0, T), :], vpair[t, pl.ds(T, T), :]], axis=1)
                    res = jnp.dot(
                        v2, jnp.concatenate([s2, s2], axis=0), preferred_element_type=F32
                    )
                    fwd_each[t] = res[:, :T] + res[:, T:] + fwd_each[idx[2, t]]
                return carry

            lax.fori_loop(0, group // UNROLL, body, 0)

        return run

    plan = [
        do_split(0), do_split(1), do_split(2), do_split(3), ev_z(1, 0),
        do_split(4), do_split(5), ev_x(0), ev_row_y, ev_z(1, 1), ev_y_first, do_split(6), do_split(7),
        ev_y(0), ev_z(2, 0), ev_z(2, 1), ev_y(-1), ev_y(1), ev_z(1, 2), ev_x(1),
        ev_z(3, 0), ev_z(3, 1), ev_z(2, 2), ev_x_end, do_gsplit,
        do_bwd(0), ev_y(-2), ev_y(2), do_bwd(1), ev_z(4, 0), do_bwd(2), ev_z(4, 1), do_bwd(3), ev_z(3, 2),
        do_bwd(4), ev_y(-3), ev_y(3), do_bwd(5), do_bwd(6), ev_z(4, 2), ev_y(-4), do_bwd(7),
    ]
    for step in plan:
        step()

    comm.phase = 1

    order = (4, -3, 3, -2, 2, -1, 1, 0)
    kinds = ((1, 0), (1, 1), (0, 0), (0, 1))
    core_got = {}
    for n, d in enumerate(order):
        slot = comm.slot()
        for m, (other, h) in enumerate(kinds):
            tile = ctile(other, d, h, 1 - core, -1)
            part[tile] = bwd_each[idx[5, tile]]
            comm.send(part.at[tile], from_core.at[4 * n + m], partner, slot=slot)
        four = from_core.at[pl.ds(4 * n, 4)]
        core_got[d] = (n, comm.copy(four, four, partner, slot).wait_recv)
    own_y, a_got, b_got = {}, {}, {}
    RPIECES = ((0, 0), (1, 0), (0, 1))

    def ring_send(p, d, sign, slot, got):
        other, h = RPIECES[p]
        got[p, slot] = comm.send(
            part.at[ctile(other, d, h)], ring.at[slot * 3 + p], za if sign > 0 else zb
        )

    def ev_merge(d):
        def run():
            n, wait = core_got[d]
            wait()
            for m, (other, h) in enumerate(kinds):
                tile = ctile(other, d, h)
                part[tile] = bwd_each[idx[5, tile]] + from_core[4 * n + m]
                if (other, h) == (1, 1):
                    own_y[d] = comm.send(part.at[tile], from_y.at[d % NZ], ypair)
                if d == 4 and h == 0:
                    ring_send(other, 4, 1, 3, a_got)
                if d == -3 and h == 0:
                    ring_send(other, -3, -1, 6, b_got)

        return run

    def ev_merge_y(d):
        def run():
            own_y[d]()
            tile = ctile(0, d, 1)
            part[tile] = part[tile] + from_y[d % NZ]
            if d == 4:
                ring_send(2, 4, 1, 3, a_got)
            if d == -3:
                ring_send(2, -3, -1, 6, b_got)

        return run

    def ev_a(p, left):
        def run():
            other, h = RPIECES[p]
            a_got[p, left]()
            tile = ctile(other, left, h)
            part[tile] = part[tile] + ring[left * 3 + p]
            if left:
                ring_send(p, left, 1, left - 1, a_got)

        return run

    def ev_b(p, left):
        def run():
            other, h = RPIECES[p]
            b_got[p, 4 + left]()
            tile = ctile(other, -left, h)
            part[tile] = part[tile] + ring[(4 + left) * 3 + p]
            if left:
                ring_send(p, -left, -1, 4 + left - 1, b_got)

        return run

    def ev_grad_y():
        own_y["end"] = comm.send(part.at[ctile(1, 0, 0)], from_y.at[NZ], ypair)

    def ev_grad(h):
        def run():
            total = part[ctile(0, 0, h)]
            if h == 0:
                own_y["end"]()
                total = total + from_y[NZ]
            cs = lax.rsqrt(cdeg[pl.ds(h, 1), :].astype(F32))
            out[2 + h] = (total * cs).T

        return run

    fa, fb = {}, {}

    def two(ref, tile):
        return ref.at[pl.ds(tile, 2)]

    def ev_f_start():
        for other in (1, 0):
            for d in (2, -1, 1, 0):
                for h in range(2):
                    tile = rtile(other, d, h)
                    fpart[tile] = fwd_each[idx[4, tile]]
                if d == 2:
                    fa[other] = comm.send(two(fpart, rtile(other, 2, 0)), two(xring, other * 2), xa, n=2)
                if d == -1:
                    fb[other] = comm.send(two(fpart, rtile(other, -1, 0)), two(xring, 4 + other * 2), xb, n=2)

    def ev_f_mid(other):
        def run():
            fa[other]()
            for h in range(2):
                tile = rtile(other, 1, h)
                fpart[tile] = fpart[tile] + xring[other * 2 + h]
            fa[other] = comm.send(two(fpart, rtile(other, 1, 0)), two(xring, 8 + other * 2), xa, n=2)

        return run

    def ev_f_last(other):
        def run():
            fb[other]()
            fa[other]()
            for h in range(2):
                tile = rtile(other, 0, h)
                fpart[tile] = fpart[tile] + (xring[4 + other * 2 + h] + xring[8 + other * 2 + h])
            if other:
                fa["y"] = comm.send(two(fpart, rtile(1, 0, 0)), two(from_yh, 0), ypeer, n=2)

        return run

    def ev_f_end():
        fa["y"]()
        for h in range(2):
            rs = lax.rsqrt(rdeg[pl.ds(h, 1), :].astype(F32))
            total = fpart[rtile(0, 0, h)] + from_yh[h]
            out[h] = (total.T * rs).T

    plan = [
        ev_core_end, ev_merge(4), ev_merge(-3), do_ssplit, ev_merge(3), ev_merge(-2), do_fwd(0),
        ev_merge(2), ev_merge(-1), ev_merge(1), ev_merge(0), do_fwd(1),
        ev_a(1, 3), ev_b(1, 2), ev_merge_y(4), do_fwd(2), ev_a(0, 3), ev_b(0, 2), ev_merge_y(-3), do_fwd(3),
        ev_merge_y(3), do_fwd(4), ev_a(2, 3), ev_merge_y(-2), do_fwd(5),
        ev_a(1, 2), ev_b(1, 1), ev_b(2, 2), do_fwd(6), ev_a(0, 2), ev_b(0, 1), ev_merge_y(2), ev_merge_y(-1), do_fwd(7),
        ev_f_start, ev_a(2, 2), ev_merge_y(1), ev_a(1, 1), ev_b(1, 0), ev_b(2, 1), ev_merge_y(0),
        ev_a(0, 1), ev_b(0, 0), ev_f_mid(1), ev_f_mid(0), ev_a(2, 1), ev_a(1, 0), ev_grad_y, ev_b(2, 0),
        ev_f_last(1), ev_a(0, 0), ev_f_last(0), ev_a(2, 0), ev_grad(1), ev_grad(0), ev_f_end,
    ]
    for step in plan:
        step()
    assert comm.tiles == [N_AG, N_RS] and comm.n == N_RECV, (comm.tiles, comm.n)
    for phase, n in ((0, N_AG), (1, N_RS)):
        comm.phase = phase
        comm.copy(fwd_each.at[pl.ds(0, n)], fwd_each.at[pl.ds(0, n)], partner, 0).wait_send()


def per_device(embed, cotangent, tile_values, tile_coords, tile_count, row_degree, col_degree):
    vmem = pl.BlockSpec(memory_space=pltpu.VMEM)
    anywhere = pl.BlockSpec(memory_space=pl.ANY)
    tile = lambda n, dtype=F32, a=T, b=T: pltpu.VMEM((n, a, b), dtype)
    ints = lambda n: pltpu.VMEM((n, T), jnp.int32)
    out = pl.pallas_call(
        kernel,
        out_shape=jax.ShapeDtypeStruct((4, T, T), F32),
        in_specs=[anywhere] * 7,
        out_specs=vmem,
        scratch_shapes=[
            pltpu.VMEM((2 * T, T), F32), pltpu.VMEM((2 * T, T), F32), ints(2), ints(2), ints(2),
            pltpu.SMEM((1, 1), jnp.int32), ints(8), pltpu.SMEM((8, T), jnp.int32),
            tile(64), tile(64, BF16, T, 2 * T), tile(SLOTS), tile(SLOTS, BF16, 2 * T, T),
            tile(SLOTS + 1), tile(SLOTS + 1), tile(64), tile(32), tile(21), tile(9),
            tile(16), tile(16, BF16, 2 * T, T), tile(16), tile(12), tile(2),
            pltpu.SemaphoreType.DMA((2,)),
            pltpu.SemaphoreType.DMA((N_RECV,)),
            pltpu.SemaphoreType.DMA((11,)),
        ],
        compiler_params=pltpu.CompilerParams(
            collective_id=0, has_side_effects=True, vmem_limit_bytes=VMEM_LIMIT
        ),
    )(
        embed, cotangent, row_degree.reshape(2, T), col_degree.reshape(2, T),
        tile_coords.reshape(2, T), tile_count, tile_values[0, 0],
    )
    return out[:2].reshape(2 * T, T), out[2:].reshape(2 * T, T)


def solution(mesh):
    return jax.shard_map(
        per_device,
        mesh=mesh,
        in_specs=(
            P(("row", "col"), None),
            P(("col", "row"), None),
            P("col", "row", None, None, None),
            P(None, "col", "row", None),
            P("col", "row"),
            P(("col", "row")),
            P(("row", "col")),
        ),
        out_specs=(P(("col", "row"), None), P(("row", "col"), None)),
        check_vma=False,
    )
```

time: 92.6 us -> 64.5 us (0.70)
  the two profiles are of different devices: /device:TPU:4 before, /device:TPU:1 now
where the time goes in v2:
time: 64.5 us; the launch traced here: 64.4 us
  Pallas kernels  61.4 us (95%)
  local copies, waits for them, and re-layouts  1.69 us (3%)
  between operations  1.29 us (2%)
    pallas_call x1, Pallas kernels, per_device(): pl.pallas_call(kernel, out_shape=jax.ShapeDtypeStruct((4, T, T), F32), in...  61.4 us
    slice x1, local copies, waits for them, and re-layouts, per_device(): return (out[:2].reshape(2 * T, T), out[2:].reshape(2 * T, T))  1.69 us

profile of v2, /device:TPU:1, one launch (start us, length us, event | category | flops | bytes accessed | tf_op | source)
XLA Modules:
  0.0 64.4 jit_solution(17028013347325837880)
XLA Ops:
  1.3 61.4 %shard_map.86 = f32[4,128,128]{2,1,0:T(8,128)} custom-call(f32[256,128]{1,0:T(8,128)} %embed_hbm.1, f32[256,128]{1,0:T(8,128)} %cot_hbm.1, s32[2,128]{1,0:T(2,128)} %bitcast.9, s32[2,128]{1,0:T(2,128)} %bitcast.10, s32[2,128]{1,0:T(2,128)} %bitcast.11, s32[1,1]{1,0:T(1,128)S(6)} %copy.9.count_hbm, f32[128,128,128]{2,1,0:T(8,128)} %bitcast.6), custom_call_target="tpu_custom_call" | custom-call | tf_op jit(solution)/shard_map/pallas_call | solution.py:453
  62.7 1.7 %fusion = (f32[2,128,128]{2,1,0:T(8,128)}, f32[2,128,128]{2,1,0:T(8,128)}) fusion(f32[4,128,128]{2,1,0:T(8,128)} %shard_map.86), kind=kLoop, calls=%fused_computation | loop fusion | bytes 524288 | tf_op jit(solution)/shard_map/slice | solution.py:475

commit v3 on v2

--- a/solution.py
+++ b/solution.py
@@ -13,33 +13,32 @@
 NX, NZ = 4, 8
 UNROLL = 16
 VMEM_LIMIT = 58 * 1024 * 1024
-N_RECV = 83
+N_RECV = 97
 N_AG = N_RS = 76
 
 
 class Comm:
     def __init__(self, send_sem, recv_sems):
         self.send_sem, self.recv_sems, self.n, self.tiles = send_sem, recv_sems, 0, [0, 0]
-        self.phase = 0
 
     def slot(self):
         self.n += 1
         return self.n - 1
 
-    def copy(self, src, dst, dev, slot):
+    def copy(self, src, dst, dev, slot, phase=0):
         return pltpu.make_async_remote_copy(
             src_ref=src,
             dst_ref=dst,
-            send_sem=self.send_sem.at[self.phase],
+            send_sem=self.send_sem.at[phase],
             recv_sem=self.recv_sems.at[slot],
             device_id=dev,
             device_id_type=MESH,
         )
 
-    def send(self, src, dst, dev, land=None, slot=None, n=1):
+    def send(self, src, dst, dev, land=None, slot=None, phase=0):
         slot = self.slot() if slot is None else slot
-        self.copy(src, dst, dev, slot).start()
-        self.tiles[self.phase] += n
+        self.copy(src, dst, dev, slot, phase).start()
+        self.tiles[phase] += 1
         return lambda: self.copy(src, dst if land is None else land, dev, slot).wait_recv()
 
 
@@ -117,20 +116,26 @@
 
     comm = Comm(send_sem, recv_sems)
 
-    def share(ref, tile, dev, land, n=1, slot=None):
-        if n > 1:
-            return comm.send(ref.at[pl.ds(tile, n)], ref.at[pl.ds(tile, n)], dev, ref.at[pl.ds(land, n)], slot, n)
-        return comm.send(ref.at[tile], ref.at[tile], dev, ref.at[land], slot)
+    def share(ref, tile, dev, land):
+        return comm.send(ref.at[tile], ref.at[tile], dev, ref.at[land])
+
+    def push(src, dst, dev, slot=None):
+        return comm.send(src, dst, dev, slot=slot, phase=1)
 
     core_slot = comm.slot()
 
     def col_core(tile):
         comm.send(panel.at[tile], panel.at[tile], partner, slot=core_slot)
 
-    got_yh = share(gpanel, rtile(0, 0, 0), ypeer, rtile(1, 0, 0), 2)
-    xa1, xb1, xa2 = {}, {}, {}
-    xa1[0] = share(gpanel, rtile(0, 0, 0), xa, rtile(0, -1, 0), 2)
-    xb1[0] = share(gpanel, rtile(0, 0, 0), xb, rtile(0, 1, 0), 2)
+    got_yh, xa1, xb1, xa2 = {}, {}, {}, {}
+
+    def x_send(other, h):
+        xa1[other, h] = share(gpanel, rtile(other, 0, h), xa, rtile(other, -1, h))
+        xb1[other, h] = share(gpanel, rtile(other, 0, h), xb, rtile(other, 1, h))
+
+    x_send(0, 0)
+    x_send(0, 1)
+    got_yh[0] = share(gpanel, rtile(0, 0, 0), ypeer, rtile(1, 0, 0))
     za_got, zb_got, y_got = {}, {}, {}
     PIECES = ((0, 0), (0, 1), (1, 0))
 
@@ -143,6 +148,7 @@
 
     z_send(0, 0)
     y_first = share(panel, ctile(0, 0, 0), ypair, ctile(1, 0, 0))
+    got_yh[1] = share(gpanel, rtile(0, 0, 1), ypeer, rtile(1, 0, 1))
     z_send(1, 0)
     y_got[0] = share(panel, ctile(0, 0, 1), ypair, ctile(1, 0, 1))
     for h in range(2):
@@ -167,22 +173,24 @@
     fwd_each[SLOTS] = jnp.zeros((T, T), F32)
     bwd_each[SLOTS] = jnp.zeros((T, T), F32)
 
-    def ev_row_y():
-        got_yh()
-        xa1[1] = share(gpanel, rtile(1, 0, 0), xa, rtile(1, -1, 0), 2)
-        xb1[1] = share(gpanel, rtile(1, 0, 0), xb, rtile(1, 1, 0), 2)
-
-    def ev_x(other):
-        def run():
-            xa1[other]()
-            xa2[other] = share(gpanel, rtile(other, -1, 0), xa, rtile(other, -2, 0), 2)
-            xb1[other]()
+    def ev_row_y(h):
+        def run():
+            got_yh[h]()
+            x_send(1, h)
+
+        return run
+
+    def ev_x(other, h):
+        def run():
+            xa1[other, h]()
+            xa2[other, h] = share(gpanel, rtile(other, -1, h), xa, rtile(other, -2, h))
+            xb1[other, h]()
 
         return run
 
     def ev_x_end():
-        xa2[0]()
-        xa2[1]()
+        for key in ((0, 0), (0, 1), (1, 0), (1, 1)):
+            xa2[key]()
 
     def ev_y_first():
         y_first()
@@ -285,36 +293,28 @@
 
         return run
 
-    plan = [
-        do_split(0), do_split(1), do_split(2), do_split(3), ev_z(1, 0),
-        do_split(4), do_split(5), ev_x(0), ev_row_y, ev_z(1, 1), ev_y_first, do_split(6), do_split(7),
-        ev_y(0), ev_z(2, 0), ev_z(2, 1), ev_y(-1), ev_y(1), ev_z(1, 2), ev_x(1),
-        ev_z(3, 0), ev_z(3, 1), ev_z(2, 2), ev_x_end, do_gsplit,
-        do_bwd(0), ev_y(-2), ev_y(2), do_bwd(1), ev_z(4, 0), do_bwd(2), ev_z(4, 1), do_bwd(3), ev_z(3, 2),
-        do_bwd(4), ev_y(-3), ev_y(3), do_bwd(5), do_bwd(6), ev_z(4, 2), ev_y(-4), do_bwd(7),
-    ]
-    for step in plan:
-        step()
-
-    comm.phase = 1
-
     order = (4, -3, 3, -2, 2, -1, 1, 0)
     kinds = ((1, 0), (1, 1), (0, 0), (0, 1))
     core_got = {}
-    for n, d in enumerate(order):
-        slot = comm.slot()
-        for m, (other, h) in enumerate(kinds):
-            tile = ctile(other, d, h, 1 - core, -1)
-            part[tile] = bwd_each[idx[5, tile]]
-            comm.send(part.at[tile], from_core.at[4 * n + m], partner, slot=slot)
-        four = from_core.at[pl.ds(4 * n, 4)]
-        core_got[d] = (n, comm.copy(four, four, partner, slot).wait_recv)
+
+    def ev_pick(d):
+        def run():
+            n, slot = order.index(d), comm.slot()
+            for m, (other, h) in enumerate(kinds):
+                tile = ctile(other, d, h, 1 - core, -1)
+                part[tile] = bwd_each[idx[5, tile]]
+                push(part.at[tile], from_core.at[4 * n + m], partner, slot)
+            four = from_core.at[pl.ds(4 * n, 4)]
+            core_got[d] = (n, lambda: comm.copy(four, four, partner, slot).wait_recv())
+
+        return run
+
     own_y, a_got, b_got = {}, {}, {}
     RPIECES = ((0, 0), (1, 0), (0, 1))
 
     def ring_send(p, d, sign, slot, got):
         other, h = RPIECES[p]
-        got[p, slot] = comm.send(
+        got[p, slot] = push(
             part.at[ctile(other, d, h)], ring.at[slot * 3 + p], za if sign > 0 else zb
         )
 
@@ -326,7 +326,7 @@
                 tile = ctile(other, d, h)
                 part[tile] = bwd_each[idx[5, tile]] + from_core[4 * n + m]
                 if (other, h) == (1, 1):
-                    own_y[d] = comm.send(part.at[tile], from_y.at[d % NZ], ypair)
+                    own_y[d] = push(part.at[tile], from_y.at[d % NZ], ypair)
                 if d == 4 and h == 0:
                     ring_send(other, 4, 1, 3, a_got)
                 if d == -3 and h == 0:
@@ -369,7 +369,7 @@
         return run
 
     def ev_grad_y():
-        own_y["end"] = comm.send(part.at[ctile(1, 0, 0)], from_y.at[NZ], ypair)
+        own_y["end"] = push(part.at[ctile(1, 0, 0)], from_y.at[NZ], ypair)
 
     def ev_grad(h):
         def run():
@@ -382,67 +382,79 @@
 
         return run
 
-    fa, fb = {}, {}
-
-    def two(ref, tile):
-        return ref.at[pl.ds(tile, 2)]
+    fa, fb, fy = {}, {}, {}
+
+    def f_a2(other, h):
+        fa[other, h] = push(fpart.at[rtile(other, 2, h)], xring.at[other * 2 + h], xa)
+
+    def f_b1(other, h):
+        fb[other, h] = push(fpart.at[rtile(other, -1, h)], xring.at[4 + other * 2 + h], xb)
 
     def ev_f_start():
-        for other in (1, 0):
-            for d in (2, -1, 1, 0):
-                for h in range(2):
-                    tile = rtile(other, d, h)
-                    fpart[tile] = fwd_each[idx[4, tile]]
+        for other, d in ((1, 2), (1, -1), (0, 2), (0, -1), (1, 1), (0, 1), (1, 0), (0, 0)):
+            for h in range(2):
+                tile = rtile(other, d, h)
+                fpart[tile] = fwd_each[idx[4, tile]]
+            for h in range(2):
                 if d == 2:
-                    fa[other] = comm.send(two(fpart, rtile(other, 2, 0)), two(xring, other * 2), xa, n=2)
-                if d == -1:
-                    fb[other] = comm.send(two(fpart, rtile(other, -1, 0)), two(xring, 4 + other * 2), xb, n=2)
-
-    def ev_f_mid(other):
-        def run():
-            fa[other]()
-            for h in range(2):
-                tile = rtile(other, 1, h)
-                fpart[tile] = fpart[tile] + xring[other * 2 + h]
-            fa[other] = comm.send(two(fpart, rtile(other, 1, 0)), two(xring, 8 + other * 2), xa, n=2)
-
-        return run
-
-    def ev_f_last(other):
-        def run():
-            fb[other]()
-            fa[other]()
-            for h in range(2):
-                tile = rtile(other, 0, h)
-                fpart[tile] = fpart[tile] + (xring[4 + other * 2 + h] + xring[8 + other * 2 + h])
+                    f_a2(other, h)
+                if (other, d) == (1, -1):
+                    f_b1(other, h)
+
+    def ev_f_mid(other, h):
+        def run():
+            fa[other, h]()
+            tile = rtile(other, 1, h)
+            fpart[tile] = fpart[tile] + xring[other * 2 + h]
+            fa[other, h] = push(fpart.at[tile], xring.at[8 + other * 2 + h], xa)
+            if (other, h) == (1, 1):
+                f_b1(0, 0)
+                f_b1(0, 1)
+
+        return run
+
+    def ev_f_last(other, h):
+        def run():
+            fb[other, h]()
+            fa[other, h]()
+            tile = rtile(other, 0, h)
+            fpart[tile] = fpart[tile] + (xring[4 + other * 2 + h] + xring[8 + other * 2 + h])
             if other:
-                fa["y"] = comm.send(two(fpart, rtile(1, 0, 0)), two(from_yh, 0), ypeer, n=2)
-
-        return run
-
-    def ev_f_end():
-        fa["y"]()
-        for h in range(2):
+                fy[h] = push(fpart.at[tile], from_yh.at[h], ypeer)
+
+        return run
+
+    def ev_f_end(h):
+        def run():
+            fy[h]()
             rs = lax.rsqrt(rdeg[pl.ds(h, 1), :].astype(F32))
             total = fpart[rtile(0, 0, h)] + from_yh[h]
             out[h] = (total.T * rs).T
 
+        return run
+
     plan = [
-        ev_core_end, ev_merge(4), ev_merge(-3), do_ssplit, ev_merge(3), ev_merge(-2), do_fwd(0),
-        ev_merge(2), ev_merge(-1), ev_merge(1), ev_merge(0), do_fwd(1),
-        ev_a(1, 3), ev_b(1, 2), ev_merge_y(4), do_fwd(2), ev_a(0, 3), ev_b(0, 2), ev_merge_y(-3), do_fwd(3),
-        ev_merge_y(3), do_fwd(4), ev_a(2, 3), ev_merge_y(-2), do_fwd(5),
-        ev_a(1, 2), ev_b(1, 1), ev_b(2, 2), do_fwd(6), ev_a(0, 2), ev_b(0, 1), ev_merge_y(2), ev_merge_y(-1), do_fwd(7),
-        ev_f_start, ev_a(2, 2), ev_merge_y(1), ev_a(1, 1), ev_b(1, 0), ev_b(2, 1), ev_merge_y(0),
-        ev_a(0, 1), ev_b(0, 0), ev_f_mid(1), ev_f_mid(0), ev_a(2, 1), ev_a(1, 0), ev_grad_y, ev_b(2, 0),
-        ev_f_last(1), ev_a(0, 0), ev_f_last(0), ev_a(2, 0), ev_grad(1), ev_grad(0), ev_f_end,
+        do_split(0), do_split(1), do_split(2), do_split(3), do_split(4), do_split(5), ev_x(0, 0), ev_z(1, 0),
+        do_split(6), do_split(7), ev_row_y(0), ev_y_first, ev_x(0, 1), ev_z(1, 1), ev_row_y(1), ev_y(0),
+        ev_z(2, 0), ev_x(1, 0), ev_y(-1), ev_z(1, 2), ev_y(1), ev_z(2, 1), ev_x(1, 1), ev_z(3, 0), ev_z(2, 2),
+        ev_x_end, do_gsplit, ev_y(-2), do_bwd(0), do_bwd(1), ev_z(3, 1), do_bwd(2), ev_z(4, 0), ev_y(2),
+        do_bwd(3), do_bwd(4), do_bwd(5), do_bwd(6), ev_z(3, 2), do_bwd(7), ev_pick(4), ev_pick(-3), ev_pick(3),
+        ev_pick(-2), ev_pick(2), ev_z(4, 1), ev_pick(-1), ev_pick(1), ev_pick(0), ev_y(-3), ev_merge(4),
+        ev_merge(-3), ev_y(3), ev_merge(3), ev_merge(-2), ev_z(4, 2), ev_merge(2), ev_merge(-1), ev_y(-4),
+        ev_merge(1), ev_merge(0), ev_a(1, 3), ev_core_end, do_ssplit, do_fwd(0), ev_merge_y(4), ev_a(0, 3),
+        do_fwd(1), do_fwd(2), do_fwd(3), do_fwd(4), do_fwd(5), do_fwd(6), do_fwd(7), ev_f_start, ev_a(1, 2),
+        ev_merge_y(3), ev_merge_y(-2), ev_a(2, 3), ev_merge_y(-3), ev_b(1, 2), ev_b(0, 2), ev_a(0, 2),
+        ev_merge_y(2), ev_merge_y(-1), ev_f_mid(1, 0), ev_a(1, 1), ev_merge_y(1), ev_f_mid(1, 1), ev_a(2, 2),
+        ev_b(2, 2), ev_merge_y(0), ev_b(1, 1), ev_f_mid(0, 0), ev_b(0, 1), ev_f_mid(0, 1), ev_a(0, 1),
+        ev_f_last(1, 0), ev_a(1, 0), ev_f_last(1, 1), ev_a(2, 1), ev_b(2, 1), ev_b(1, 0), ev_grad_y,
+        ev_f_last(0, 0), ev_b(0, 0), ev_f_last(0, 1), ev_a(0, 0), ev_a(2, 0), ev_f_end(0), ev_b(2, 0),
+        ev_grad(1), ev_f_end(1), ev_grad(0),
     ]
     for step in plan:
         step()
     assert comm.tiles == [N_AG, N_RS] and comm.n == N_RECV, (comm.tiles, comm.n)
     for phase, n in ((0, N_AG), (1, N_RS)):
-        comm.phase = phase
-        comm.copy(fwd_each.at[pl.ds(0, n)], fwd_each.at[pl.ds(0, n)], partner, 0).wait_send()
+        comm.copy(fwd_each.at[pl.ds(0, n)], fwd_each.at[pl.ds(0, n)], partner, 0, phase).wait_send()
 
 
 def per_device(embed, cotangent, tile_values, tile_coords, tile_count, row_degree, col_degree):

time: 64.5 us -> 56.8 us (0.88)
  Pallas kernels: 61.4 us -> 53.7 us
    pallas_call x1, Pallas kernels: 61.4 us -> 53.7 us  [per_device(): pl.pallas_call(kernel, out_shape=jax.ShapeDtypeStruct((4, T, T), F32), in...]
where the time goes in v3:
time: 56.8 us; the launch traced here: 56.7 us
  Pallas kernels  53.7 us (95%)
  local copies, waits for them, and re-layouts  1.69 us (3%)
  between operations  1.29 us (2%)
    pallas_call x1, Pallas kernels, per_device(): pl.pallas_call(kernel, out_shape=jax.ShapeDtypeStruct((4, T, T), F32), in...  53.7 us
    slice x1, local copies, waits for them, and re-layouts, per_device(): return (out[:2].reshape(2 * T, T), out[2:].reshape(2 * T, T))  1.69 us

profile of v3, /device:TPU:1, one launch (start us, length us, event | category | flops | bytes accessed | tf_op | source)
XLA Modules:
  0.0 56.7 jit_solution(15852161488452554994)
XLA Ops:
  1.3 53.7 %shard_map.86 = f32[4,128,128]{2,1,0:T(8,128)} custom-call(f32[256,128]{1,0:T(8,128)} %embed_hbm.1, f32[256,128]{1,0:T(8,128)} %cot_hbm.1, s32[2,128]{1,0:T(2,128)} %bitcast.9, s32[2,128]{1,0:T(2,128)} %bitcast.10, s32[2,128]{1,0:T(2,128)} %bitcast.11, s32[1,1]{1,0:T(1,128)S(6)} %copy.9.count_hbm, f32[128,128,128]{2,1,0:T(8,128)} %bitcast.6), custom_call_target="tpu_custom_call" | custom-call | tf_op jit(solution)/shard_map/pallas_call | solution.py:465
  55.0 1.7 %fusion = (f32[2,128,128]{2,1,0:T(8,128)}, f32[2,128,128]{2,1,0:T(8,128)}) fusion(f32[4,128,128]{2,1,0:T(8,128)} %shard_map.86), kind=kLoop, calls=%fused_computation | loop fusion | bytes 524288 | tf_op jit(solution)/shard_map/slice | solution.py:487

commit v4 on v3

--- a/solution.py
+++ b/solution.py
@@ -12,7 +12,7 @@
 SLOTS = 128
 NX, NZ = 4, 8
 UNROLL = 16
-VMEM_LIMIT = 58 * 1024 * 1024
+VMEM_LIMIT = 53 * 1024 * 1024
 N_RECV = 97
 N_AG = N_RS = 76
 
@@ -49,11 +49,11 @@
 
 def kernel(
     embed_hbm, cot_hbm, rdeg_hbm, cdeg_hbm, coords_hbm, count_hbm, values,
-    out,
+    out_hbm,
     embed, cot, rdeg, cdeg, coords, count, table, idx,
     panel, pairs, vraw, vpair, fwd_each, bwd_each, part, from_core, ring, from_y,
     gpanel, gpair, fpart, xring, from_yh,
-    send_sem, recv_sems, load_sems,
+    out, send_sem, recv_sems, load_sems,
 ):
     row, col = lax.axis_index("row"), lax.axis_index("col")
     x, yh = lax.div(row, 2), lax.rem(row, 2)
@@ -135,6 +135,7 @@
 
     x_send(0, 0)
     x_send(0, 1)
+    y_first = share(panel, ctile(0, 0, 0), ypair, ctile(1, 0, 0))
     got_yh[0] = share(gpanel, rtile(0, 0, 0), ypeer, rtile(1, 0, 0))
     za_got, zb_got, y_got = {}, {}, {}
     PIECES = ((0, 0), (0, 1), (1, 0))
@@ -146,10 +147,9 @@
         if k < 3:
             zb_got[k + 1, p] = share(panel, ctile(other, k, h), zb, ctile(other, k + 1, h))
 
-    z_send(0, 0)
-    y_first = share(panel, ctile(0, 0, 0), ypair, ctile(1, 0, 0))
     got_yh[1] = share(gpanel, rtile(0, 0, 1), ypeer, rtile(1, 0, 1))
     z_send(1, 0)
+    z_send(0, 0)
     y_got[0] = share(panel, ctile(0, 0, 1), ypair, ctile(1, 0, 1))
     for h in range(2):
         col_core(ctile(0, 0, h))
@@ -368,6 +368,11 @@
 
         return run
 
+    def finish(n):
+        copy = pltpu.make_async_copy(out.at[n], out_hbm.at[n], load_sems.at[n])
+        copy.start()
+        finished.append(copy)
+
     def ev_grad_y():
         own_y["end"] = push(part.at[ctile(1, 0, 0)], from_y.at[NZ], ypair)
 
@@ -379,6 +384,7 @@
                 total = total + from_y[NZ]
             cs = lax.rsqrt(cdeg[pl.ds(h, 1), :].astype(F32))
             out[2 + h] = (total * cs).T
+            finish(2 + h)
 
         return run
 
@@ -430,49 +436,55 @@
             rs = lax.rsqrt(rdeg[pl.ds(h, 1), :].astype(F32))
             total = fpart[rtile(0, 0, h)] + from_yh[h]
             out[h] = (total.T * rs).T
-
-        return run
+            finish(h)
+
+        return run
+
+    finished = []
 
     plan = [
-        do_split(0), do_split(1), do_split(2), do_split(3), do_split(4), do_split(5), ev_x(0, 0), ev_z(1, 0),
-        do_split(6), do_split(7), ev_row_y(0), ev_y_first, ev_x(0, 1), ev_z(1, 1), ev_row_y(1), ev_y(0),
-        ev_z(2, 0), ev_x(1, 0), ev_y(-1), ev_z(1, 2), ev_y(1), ev_z(2, 1), ev_x(1, 1), ev_z(3, 0), ev_z(2, 2),
-        ev_x_end, do_gsplit, ev_y(-2), do_bwd(0), do_bwd(1), ev_z(3, 1), do_bwd(2), ev_z(4, 0), ev_y(2),
-        do_bwd(3), do_bwd(4), do_bwd(5), do_bwd(6), ev_z(3, 2), do_bwd(7), ev_pick(4), ev_pick(-3), ev_pick(3),
-        ev_pick(-2), ev_pick(2), ev_z(4, 1), ev_pick(-1), ev_pick(1), ev_pick(0), ev_y(-3), ev_merge(4),
-        ev_merge(-3), ev_y(3), ev_merge(3), ev_merge(-2), ev_z(4, 2), ev_merge(2), ev_merge(-1), ev_y(-4),
-        ev_merge(1), ev_merge(0), ev_a(1, 3), ev_core_end, do_ssplit, do_fwd(0), ev_merge_y(4), ev_a(0, 3),
-        do_fwd(1), do_fwd(2), do_fwd(3), do_fwd(4), do_fwd(5), do_fwd(6), do_fwd(7), ev_f_start, ev_a(1, 2),
-        ev_merge_y(3), ev_merge_y(-2), ev_a(2, 3), ev_merge_y(-3), ev_b(1, 2), ev_b(0, 2), ev_a(0, 2),
-        ev_merge_y(2), ev_merge_y(-1), ev_f_mid(1, 0), ev_a(1, 1), ev_merge_y(1), ev_f_mid(1, 1), ev_a(2, 2),
-        ev_b(2, 2), ev_merge_y(0), ev_b(1, 1), ev_f_mid(0, 0), ev_b(0, 1), ev_f_mid(0, 1), ev_a(0, 1),
-        ev_f_last(1, 0), ev_a(1, 0), ev_f_last(1, 1), ev_a(2, 1), ev_b(2, 1), ev_b(1, 0), ev_grad_y,
-        ev_f_last(0, 0), ev_b(0, 0), ev_f_last(0, 1), ev_a(0, 0), ev_a(2, 0), ev_f_end(0), ev_b(2, 0),
-        ev_grad(1), ev_f_end(1), ev_grad(0),
+        ev_y_first, ev_z(1, 1), ev_x(0, 0), ev_z(1, 0), do_split(0), ev_row_y(0), do_split(1), ev_z(1, 2),
+        ev_row_y(1), ev_z(2, 1), do_split(2), do_split(3), ev_x(0, 1), do_split(4), ev_x(1, 0), ev_z(2, 0),
+        do_split(5), do_split(6), ev_y(0), do_split(7), ev_x(1, 1), ev_z(2, 2), ev_z(3, 1), ev_y(-1), ev_y(2),
+        ev_y(1), ev_y(-2), ev_x_end, do_gsplit, do_bwd(0), do_bwd(1), ev_z(3, 0), do_bwd(2), ev_z(3, 2),
+        do_bwd(3), ev_z(4, 1), do_bwd(4), ev_y(-3), do_bwd(5), do_bwd(6), do_bwd(7), ev_pick(4), ev_pick(-3),
+        ev_y(3), ev_pick(3), ev_z(4, 0), ev_merge(4), ev_z(4, 2), ev_y(-4), ev_pick(-2), ev_merge(-3),
+        ev_pick(2), ev_merge(3), ev_core_end, do_ssplit, do_fwd(0), do_fwd(1), do_fwd(2), do_fwd(3), ev_a(1, 3),
+        do_fwd(4), ev_merge_y(4), do_fwd(5), ev_a(0, 3), do_fwd(6), do_fwd(7), ev_f_start, ev_merge(-2),
+        ev_merge_y(-3), ev_pick(-1), ev_merge_y(3), ev_b(0, 2), ev_merge(2), ev_b(1, 2), ev_merge(-1),
+        ev_pick(1), ev_a(2, 3), ev_a(1, 2), ev_pick(0), ev_merge(1), ev_a(0, 2), ev_merge_y(-2), ev_f_mid(1, 0),
+        ev_f_mid(1, 1), ev_b(2, 2), ev_merge_y(2), ev_b(1, 1), ev_merge(0), ev_a(2, 2), ev_a(1, 1),
+        ev_f_last(1, 0), ev_merge_y(-1), ev_b(0, 1), ev_b(2, 1), ev_merge_y(1), ev_f_last(1, 1), ev_f_mid(0, 0),
+        ev_a(0, 1), ev_f_mid(0, 1), ev_b(1, 0), ev_a(2, 1), ev_merge_y(0), ev_a(1, 0), ev_grad_y, ev_a(0, 0),
+        ev_b(2, 0), ev_f_last(0, 1), ev_b(0, 0), ev_f_last(0, 0), ev_f_end(0), ev_a(2, 0), ev_grad(1),
+        ev_f_end(1), ev_grad(0),
     ]
     for step in plan:
         step()
+    for copy in finished:
+        copy.wait()
     assert comm.tiles == [N_AG, N_RS] and comm.n == N_RECV, (comm.tiles, comm.n)
     for phase, n in ((0, N_AG), (1, N_RS)):
         comm.copy(fwd_each.at[pl.ds(0, n)], fwd_each.at[pl.ds(0, n)], partner, 0, phase).wait_send()
 
 
 def per_device(embed, cotangent, tile_values, tile_coords, tile_count, row_degree, col_degree):
-    vmem = pl.BlockSpec(memory_space=pltpu.VMEM)
     anywhere = pl.BlockSpec(memory_space=pl.ANY)
+    hbm = lambda a: pltpu.with_memory_space_constraint(a, pltpu.HBM)
     tile = lambda n, dtype=F32, a=T, b=T: pltpu.VMEM((n, a, b), dtype)
     ints = lambda n: pltpu.VMEM((n, T), jnp.int32)
     out = pl.pallas_call(
         kernel,
         out_shape=jax.ShapeDtypeStruct((4, T, T), F32),
         in_specs=[anywhere] * 7,
-        out_specs=vmem,
+        out_specs=anywhere,
         scratch_shapes=[
             pltpu.VMEM((2 * T, T), F32), pltpu.VMEM((2 * T, T), F32), ints(2), ints(2), ints(2),
             pltpu.SMEM((1, 1), jnp.int32), ints(8), pltpu.SMEM((8, T), jnp.int32),
             tile(64), tile(64, BF16, T, 2 * T), tile(SLOTS), tile(SLOTS, BF16, 2 * T, T),
             tile(SLOTS + 1), tile(SLOTS + 1), tile(64), tile(32), tile(21), tile(9),
             tile(16), tile(16, BF16, 2 * T, T), tile(16), tile(12), tile(2),
+            tile(4),
             pltpu.SemaphoreType.DMA((2,)),
             pltpu.SemaphoreType.DMA((N_RECV,)),
             pltpu.SemaphoreType.DMA((11,)),
@@ -481,8 +493,8 @@
             collective_id=0, has_side_effects=True, vmem_limit_bytes=VMEM_LIMIT
         ),
     )(
-        embed, cotangent, row_degree.reshape(2, T), col_degree.reshape(2, T),
-        tile_coords.reshape(2, T), tile_count, tile_values[0, 0],
+        hbm(embed), hbm(cotangent), hbm(row_degree.reshape(2, T)), hbm(col_degree.reshape(2, T)),
+        hbm(tile_coords.reshape(2, T)), tile_count, hbm(tile_values[0, 0]),
     )
     return out[:2].reshape(2 * T, T), out[2:].reshape(2 * T, T)
 

time: 56.8 us -> 54.6 us (0.961)
  the two profiles are of different devices: /device:TPU:1 before, /device:TPU:2 now
where the time goes in v4:
time: 54.6 us; the launch traced here: 54.5 us
  Pallas kernels  52.5 us (96%)
  between operations  1.29 us (2%)
  local copies, waits for them, and re-layouts  0.72 us (1%)
    pallas_call x1, Pallas kernels, per_device(): pl.pallas_call(kernel, out_shape=jax.ShapeDtypeStruct((4, T, T), F32), in...  52.5 us

profile of v4, /device:TPU:2, one launch (start us, length us, event | category | flops | bytes accessed | tf_op | source)
XLA Modules:
  0.0 54.5 jit_solution(18415971340015600311)
XLA Ops:
  1.3 52.5 %shard_map.86 = f32[4,128,128]{2,1,0:T(8,128)S(1)} custom-call(f32[256,128]{1,0:T(8,128)} %embed_hbm.1, f32[256,128]{1,0:T(8,128)} %cot_hbm.1, s32[2,128]{1,0:T(2,128)} %bitcast.9, s32[2,128]{1,0:T(2,128)} %bitcast.10, s32[2,128]{1,0:T(2,128)} %bitcast.11, s32[1,1]{1,0:T(1,128)S(6)} %copy.9.count_hbm, f32[128,128,128]{2,1,0:T(8,128)} %bitcast.6), custom_call_target="tpu_custom_call" | custom-call | tf_op jit(solution)/shard_map/pallas_call | solution.py:476
  53.8 0.7 %fusion = (f32[2,128,128]{2,1,0:T(8,128)}, f32[2,128,128]{2,1,0:T(8,128)}) fusion(f32[4,128,128]{2,1,0:T(8,128)S(1)} %shard_map.86), kind=kLoop, calls=%fused_computation | loop fusion | bytes 524288 | tf_op jit(solution)/shard_map/slice | solution.py:499

commit v5 on v4

--- a/solution.py
+++ b/solution.py
@@ -443,21 +443,21 @@
     finished = []
 
     plan = [
-        ev_y_first, ev_z(1, 1), ev_x(0, 0), ev_z(1, 0), do_split(0), ev_row_y(0), do_split(1), ev_z(1, 2),
-        ev_row_y(1), ev_z(2, 1), do_split(2), do_split(3), ev_x(0, 1), do_split(4), ev_x(1, 0), ev_z(2, 0),
-        do_split(5), do_split(6), ev_y(0), do_split(7), ev_x(1, 1), ev_z(2, 2), ev_z(3, 1), ev_y(-1), ev_y(2),
-        ev_y(1), ev_y(-2), ev_x_end, do_gsplit, do_bwd(0), do_bwd(1), ev_z(3, 0), do_bwd(2), ev_z(3, 2),
-        do_bwd(3), ev_z(4, 1), do_bwd(4), ev_y(-3), do_bwd(5), do_bwd(6), do_bwd(7), ev_pick(4), ev_pick(-3),
-        ev_y(3), ev_pick(3), ev_z(4, 0), ev_merge(4), ev_z(4, 2), ev_y(-4), ev_pick(-2), ev_merge(-3),
-        ev_pick(2), ev_merge(3), ev_core_end, do_ssplit, do_fwd(0), do_fwd(1), do_fwd(2), do_fwd(3), ev_a(1, 3),
-        do_fwd(4), ev_merge_y(4), do_fwd(5), ev_a(0, 3), do_fwd(6), do_fwd(7), ev_f_start, ev_merge(-2),
-        ev_merge_y(-3), ev_pick(-1), ev_merge_y(3), ev_b(0, 2), ev_merge(2), ev_b(1, 2), ev_merge(-1),
-        ev_pick(1), ev_a(2, 3), ev_a(1, 2), ev_pick(0), ev_merge(1), ev_a(0, 2), ev_merge_y(-2), ev_f_mid(1, 0),
-        ev_f_mid(1, 1), ev_b(2, 2), ev_merge_y(2), ev_b(1, 1), ev_merge(0), ev_a(2, 2), ev_a(1, 1),
-        ev_f_last(1, 0), ev_merge_y(-1), ev_b(0, 1), ev_b(2, 1), ev_merge_y(1), ev_f_last(1, 1), ev_f_mid(0, 0),
-        ev_a(0, 1), ev_f_mid(0, 1), ev_b(1, 0), ev_a(2, 1), ev_merge_y(0), ev_a(1, 0), ev_grad_y, ev_a(0, 0),
-        ev_b(2, 0), ev_f_last(0, 1), ev_b(0, 0), ev_f_last(0, 0), ev_f_end(0), ev_a(2, 0), ev_grad(1),
-        ev_f_end(1), ev_grad(0),
+        ev_y_first, ev_z(1, 1), do_split(0), ev_z(1, 0), ev_row_y(0), do_split(1), ev_row_y(1), ev_z(1, 2),
+        ev_x(0, 1), do_split(2), ev_x(0, 0), ev_y(0), do_split(3), do_split(4), ev_z(2, 1), ev_x(1, 0),
+        ev_z(2, 0), do_split(5), ev_x(1, 1), ev_y(-1), ev_z(2, 2), ev_z(3, 1), ev_y(-2), ev_y(1), do_split(6),
+        do_split(7), ev_x_end, do_gsplit, ev_z(3, 0), do_bwd(0), do_bwd(1), do_bwd(2), do_bwd(3), ev_z(3, 2),
+        do_bwd(4), do_bwd(5), ev_z(4, 1), do_bwd(6), do_bwd(7), ev_pick(4), ev_pick(-3), ev_pick(3), ev_y(2),
+        ev_y(3), ev_merge(4), ev_pick(-2), ev_merge(3), ev_y(-3), ev_z(4, 0), ev_merge(-3), ev_z(4, 2),
+        ev_y(-4), ev_merge(-2), ev_pick(2), ev_pick(-1), ev_core_end, do_ssplit, do_fwd(0), do_fwd(1),
+        ev_a(1, 3), do_fwd(2), ev_merge_y(4), do_fwd(3), do_fwd(4), ev_a(0, 3), do_fwd(5), do_fwd(6), do_fwd(7),
+        ev_f_start, ev_b(1, 2), ev_merge_y(-3), ev_pick(1), ev_b(0, 2), ev_merge_y(3), ev_merge(2), ev_a(2, 3),
+        ev_a(1, 2), ev_pick(0), ev_merge(-1), ev_a(0, 2), ev_merge(1), ev_f_mid(1, 0), ev_merge(0),
+        ev_merge_y(-2), ev_b(2, 2), ev_b(1, 1), ev_f_mid(1, 1), ev_merge_y(2), ev_merge_y(-1), ev_a(2, 2),
+        ev_f_mid(0, 1), ev_a(1, 1), ev_f_last(1, 0), ev_merge_y(1), ev_a(0, 1), ev_f_last(1, 1), ev_b(2, 1),
+        ev_b(1, 0), ev_merge_y(0), ev_a(2, 1), ev_f_mid(0, 0), ev_b(0, 1), ev_a(1, 0), ev_grad_y, ev_a(2, 0),
+        ev_a(0, 0), ev_f_last(0, 0), ev_f_last(0, 1), ev_b(2, 0), ev_grad(1), ev_f_end(0), ev_f_end(1),
+        ev_b(0, 0), ev_grad(0),
     ]
     for step in plan:
         step()

time: 54.6 us -> 53.4 us (0.978)
  the two profiles are of different devices: /device:TPU:2 before, /device:TPU:1 now
where the time goes in v5:
time: 53.4 us; the launch traced here: 53.2 us
  Pallas kernels  51.2 us (96%)
  between operations  1.29 us (2%)
  local copies, waits for them, and re-layouts  0.72 us (1%)
    pallas_call x1, Pallas kernels, per_device(): pl.pallas_call(kernel, out_shape=jax.ShapeDtypeStruct((4, T, T), F32), in...  51.2 us

profile of v5, /device:TPU:1, one launch (start us, length us, event | category | flops | bytes accessed | tf_op | source)
XLA Modules:
  0.0 53.2 jit_solution(14947450021911422001)
XLA Ops:
  1.3 51.2 %shard_map.86 = f32[4,128,128]{2,1,0:T(8,128)S(1)} custom-call(f32[256,128]{1,0:T(8,128)} %embed_hbm.1, f32[256,128]{1,0:T(8,128)} %cot_hbm.1, s32[2,128]{1,0:T(2,128)} %bitcast.9, s32[2,128]{1,0:T(2,128)} %bitcast.10, s32[2,128]{1,0:T(2,128)} %bitcast.11, s32[1,1]{1,0:T(1,128)S(6)} %copy.9.count_hbm, f32[128,128,128]{2,1,0:T(8,128)} %bitcast.6), custom_call_target="tpu_custom_call" | custom-call | tf_op jit(solution)/shard_map/pallas_call | solution.py:476
  52.5 0.7 %fusion = (f32[2,128,128]{2,1,0:T(8,128)}, f32[2,128,128]{2,1,0:T(8,128)}) fusion(f32[4,128,128]{2,1,0:T(8,128)S(1)} %shard_map.86), kind=kLoop, calls=%fused_computation | loop fusion | bytes 524288 | tf_op jit(solution)/shard_map/slice | solution.py:499

commit v6 on v5

--- a/solution.py
+++ b/solution.py
@@ -443,21 +443,21 @@
     finished = []
 
     plan = [
-        ev_y_first, ev_z(1, 1), do_split(0), ev_z(1, 0), ev_row_y(0), do_split(1), ev_row_y(1), ev_z(1, 2),
-        ev_x(0, 1), do_split(2), ev_x(0, 0), ev_y(0), do_split(3), do_split(4), ev_z(2, 1), ev_x(1, 0),
-        ev_z(2, 0), do_split(5), ev_x(1, 1), ev_y(-1), ev_z(2, 2), ev_z(3, 1), ev_y(-2), ev_y(1), do_split(6),
-        do_split(7), ev_x_end, do_gsplit, ev_z(3, 0), do_bwd(0), do_bwd(1), do_bwd(2), do_bwd(3), ev_z(3, 2),
-        do_bwd(4), do_bwd(5), ev_z(4, 1), do_bwd(6), do_bwd(7), ev_pick(4), ev_pick(-3), ev_pick(3), ev_y(2),
-        ev_y(3), ev_merge(4), ev_pick(-2), ev_merge(3), ev_y(-3), ev_z(4, 0), ev_merge(-3), ev_z(4, 2),
-        ev_y(-4), ev_merge(-2), ev_pick(2), ev_pick(-1), ev_core_end, do_ssplit, do_fwd(0), do_fwd(1),
-        ev_a(1, 3), do_fwd(2), ev_merge_y(4), do_fwd(3), do_fwd(4), ev_a(0, 3), do_fwd(5), do_fwd(6), do_fwd(7),
-        ev_f_start, ev_b(1, 2), ev_merge_y(-3), ev_pick(1), ev_b(0, 2), ev_merge_y(3), ev_merge(2), ev_a(2, 3),
-        ev_a(1, 2), ev_pick(0), ev_merge(-1), ev_a(0, 2), ev_merge(1), ev_f_mid(1, 0), ev_merge(0),
-        ev_merge_y(-2), ev_b(2, 2), ev_b(1, 1), ev_f_mid(1, 1), ev_merge_y(2), ev_merge_y(-1), ev_a(2, 2),
-        ev_f_mid(0, 1), ev_a(1, 1), ev_f_last(1, 0), ev_merge_y(1), ev_a(0, 1), ev_f_last(1, 1), ev_b(2, 1),
-        ev_b(1, 0), ev_merge_y(0), ev_a(2, 1), ev_f_mid(0, 0), ev_b(0, 1), ev_a(1, 0), ev_grad_y, ev_a(2, 0),
-        ev_a(0, 0), ev_f_last(0, 0), ev_f_last(0, 1), ev_b(2, 0), ev_grad(1), ev_f_end(0), ev_f_end(1),
-        ev_b(0, 0), ev_grad(0),
+        ev_y_first, do_split(0), ev_z(1, 1), do_split(1), ev_x(0, 1), do_split(2), ev_z(1, 0), ev_row_y(0),
+        ev_row_y(1), do_split(3), ev_z(1, 2), do_split(4), ev_z(2, 1), do_split(5), ev_x(0, 0), ev_x(1, 0),
+        do_split(6), ev_z(2, 0), ev_x(1, 1), ev_z(2, 2), ev_y(-2), ev_y(2), ev_y(-1), do_split(7), ev_y(0),
+        ev_z(3, 1), ev_x_end, do_gsplit, do_bwd(0), do_bwd(1), do_bwd(2), ev_z(3, 0), do_bwd(3), do_bwd(4),
+        do_bwd(5), ev_z(3, 2), do_bwd(6), do_bwd(7), ev_z(4, 1), ev_y(1), ev_pick(4), ev_y(-3), ev_pick(-3),
+        ev_y(3), ev_pick(3), ev_merge(4), ev_z(4, 2), ev_merge(-3), ev_pick(-2), ev_z(4, 0), ev_y(-4),
+        ev_pick(2), ev_pick(-1), ev_pick(1), ev_merge(3), ev_merge(-2), ev_core_end, do_ssplit, ev_a(1, 3),
+        do_fwd(0), do_fwd(1), ev_merge_y(4), do_fwd(2), do_fwd(3), do_fwd(4), ev_a(0, 3), do_fwd(5), ev_b(1, 2),
+        do_fwd(6), do_fwd(7), ev_f_start, ev_merge(2), ev_merge(1), ev_a(1, 2), ev_merge_y(3), ev_a(2, 3),
+        ev_pick(0), ev_merge_y(-3), ev_b(0, 2), ev_a(0, 2), ev_merge(-1), ev_merge_y(-2), ev_merge_y(2),
+        ev_f_mid(1, 0), ev_b(1, 1), ev_a(2, 2), ev_f_mid(1, 1), ev_merge(0), ev_b(2, 2), ev_a(1, 1),
+        ev_f_last(1, 0), ev_f_mid(0, 1), ev_b(0, 1), ev_merge_y(-1), ev_f_last(1, 1), ev_merge_y(1),
+        ev_merge_y(0), ev_a(2, 1), ev_b(2, 1), ev_b(1, 0), ev_f_mid(0, 0), ev_a(1, 0), ev_a(0, 1), ev_grad_y,
+        ev_a(2, 0), ev_f_last(0, 1), ev_b(0, 0), ev_f_last(0, 0), ev_b(2, 0), ev_f_end(0), ev_grad(1),
+        ev_a(0, 0), ev_f_end(1), ev_grad(0),
     ]
     for step in plan:
         step()

time: 53.4 us -> 54.5 us (1.021)
  Pallas kernels: 51.2 us -> 52.4 us
    pallas_call x1, Pallas kernels: 51.2 us -> 52.4 us  [per_device(): pl.pallas_call(kernel, out_shape=jax.ShapeDtypeStruct((4, T, T), F32), in...]
where the time goes in v6:
time: 54.5 us; the launch traced here: 54.4 us
  Pallas kernels  52.4 us (96%)
  between operations  1.29 us (2%)
  local copies, waits for them, and re-layouts  0.72 us (1%)
    pallas_call x1, Pallas kernels, per_device(): pl.pallas_call(kernel, out_shape=jax.ShapeDtypeStruct((4, T, T), F32), in...  52.4 us

profile of v6, /device:TPU:1, one launch (start us, length us, event | category | flops | bytes accessed | tf_op | source)
XLA Modules:
  0.0 54.4 jit_solution(17482745351498486601)
XLA Ops:
  1.3 52.4 %shard_map.86 = f32[4,128,128]{2,1,0:T(8,128)S(1)} custom-call(f32[256,128]{1,0:T(8,128)} %embed_hbm.1, f32[256,128]{1,0:T(8,128)} %cot_hbm.1, s32[2,128]{1,0:T(2,128)} %bitcast.9, s32[2,128]{1,0:T(2,128)} %bitcast.10, s32[2,128]{1,0:T(2,128)} %bitcast.11, s32[1,1]{1,0:T(1,128)S(6)} %copy.9.count_hbm, f32[128,128,128]{2,1,0:T(8,128)} %bitcast.6), custom_call_target="tpu_custom_call" | custom-call | tf_op jit(solution)/shard_map/pallas_call | solution.py:476
  53.7 0.7 %fusion = (f32[2,128,128]{2,1,0:T(8,128)}, f32[2,128,128]{2,1,0:T(8,128)}) fusion(f32[4,128,128]{2,1,0:T(8,128)S(1)} %shard_map.86), kind=kLoop, calls=%fused_computation | loop fusion | bytes 524288 | tf_op jit(solution)/shard_map/slice | solution.py:499
